TPU v7x, 128 devices: a whole 4x4x4 slice. The times are simulated.
128 devices in a mesh: group: 2 (over x_hi), dev: 64 (over z, x_lo, y, core).
Axes of the slice: x: 4 (x_hi: 2, x_lo: 2; x = x_hi * 2 + x_lo), y: 4, z: 4, core: 2. Of those that a mesh axis runs over, the one named last changes fastest.
Arguments:
- query_latent: bfloat16 [512, 128, 512], P(('group', 'dev')), may hold values from -100 to 100
- query_rope: bfloat16 [512, 128, 64], P(('group', 'dev')), may hold values from -3 to 3
- cache_latent: bfloat16 [512, 2048, 512], P(('group', 'dev')), may hold values from -6 to 6
- cache_rope: bfloat16 [512, 64, 2048], P(('group', 'dev')), may hold values from -6 to 6
- lengths: int32 [512], P(('group', 'dev')), may hold values from 256 to 2048
- value_up: bfloat16 [128, 512, 128], P('dev'), may hold values from -0.25 to 0.25
- out_proj: bfloat16 [16384, 7168], P('dev'), may hold values from -0.046875 to 0.046875
- residual: bfloat16 [512, 7168], P(('group', 'dev')), may hold values from -6 to 6
- norm_gain: float32 [7168], replicated, may hold values from 0.25 to 1.75
- expert_ids: int32 [512, 8], P(('group', 'dev')), may hold values from 0 to 31, all different within a row; in each aligned block of 4 rows (0 to 3, 4 to 7, ...) at most 2 rows name the same one
- gate_values: float32 [512, 8], P(('group', 'dev')), may hold values from 0.1 to 1
- w_gate: bfloat16 [64, 7168, 512], P('dev', None, 'group'), may hold values from -0.0625 to 0.0625
- w_up: bfloat16 [64, 7168, 512], P('dev', None, 'group'), may hold values from -0.0625 to 0.0625
- w_down: bfloat16 [64, 512, 7168], P('dev', 'group'), may hold values from -0.1875 to 0.1875
Outputs:
- layer_out: bfloat16 [512, 7168], P(('group', 'dev'))
Inputs may be any that keep to these rules, and one draw needn't show every extreme that they name: `expert_ids`: each row names 8 different experts. Among the rows of one device no expert is named by more than 2 rows, and in every draw some expert is named by exactly 2 rows of some device.
All inputs are finite; a program needn't handle non-finite values.
Results may differ from a plain program's by a relative error of at most 0.008.
Values may be sent and summed in bfloat16 or wider, within the bound.
A program may use at most 128 MiB of HBM per device.

v0:
```python
import jax
import jax.numpy as jnp
from jax import lax
from jax.sharding import Mesh
from jax.sharding import PartitionSpec as P

DEV = ("dev_0", "dev_1", "dev_2", "dev_3")
GROUP_DEV = ("group", "dev_0", "dev_1", "dev_2", "dev_3")


softmax_scale = 192.0 ** (-0.5)


def split_up(array, dim, size):
    lengths = array.shape
    tiles = array.reshape(*lengths[:dim], size, lengths[dim] // size, *lengths[dim + 1 :])
    return jnp.moveaxis(tiles, dim, 0)


def sent_and_summed(array, axis, dim):
    size = lax.axis_size(axis)
    tiles = lax.all_to_all(split_up(array, dim, size), axis, 0, 0, tiled=True)
    return jnp.sum(tiles, axis=0)


def sum_by_axis(array, axes, dim):
    far, near = axes
    own = sent_and_summed(split_up(array, dim, lax.axis_size(far)), near, dim + 1)
    return jnp.sum(lax.all_to_all(own, far, 0, 0, tiled=True), axis=0)


def attend(query_latent, query_rope, cache_latent, cache_rope, lengths):
    scores = jnp.einsum(
        "thl,tcl->thc", query_latent, cache_latent, preferred_element_type=jnp.float32
    )
    scores = scores + jnp.einsum(
        "thr,trc->thc", query_rope, cache_rope, preferred_element_type=jnp.float32
    )
    scores = scores * softmax_scale
    positions = lax.broadcasted_iota(jnp.int32, scores.shape, 2)
    scores = jnp.where(positions < lengths[:, None, None], scores, -jnp.inf)
    row_peak = jnp.max(scores, axis=2, keepdims=True)
    weights = jnp.exp(scores - row_peak)
    attn_weights = (weights / jnp.sum(weights, axis=2, keepdims=True)).astype(jnp.bfloat16)
    return jnp.einsum(
        "thc,tcl->thl", attn_weights, cache_latent, preferred_element_type=jnp.float32
    ).astype(jnp.bfloat16)


def expert_rows(token_rows, w_gate, w_up, w_down):
    gate_part = jnp.dot(token_rows, w_gate[0], preferred_element_type=jnp.float32)
    up_part = jnp.dot(token_rows, w_up[0], preferred_element_type=jnp.float32)
    active = (jax.nn.silu(gate_part) * up_part).astype(jnp.bfloat16)
    return jnp.dot(active, w_down[0], preferred_element_type=jnp.float32)


def local(
    query_latent,
    query_rope,
    cache_latent,
    cache_rope,
    lengths,
    value_up,
    out_proj,
    residual,
    norm_gain,
    expert_ids,
    gate_values,
    w_gate,
    w_up,
    w_down,
):
    tok_rows = query_latent.shape[0]
    feature_width = residual.shape[1]
    mixed_latent = attend(query_latent, query_rope, cache_latent, cache_rope, lengths)
    by_head = lax.all_to_all(mixed_latent, DEV, split_axis=1, concat_axis=0, tiled=True)
    head_values = jnp.einsum(
        "thl,hlv->thv", by_head, value_up, preferred_element_type=jnp.float32
    ).astype(jnp.bfloat16)
    flat_values = head_values.reshape(head_values.shape[0], -1)
    attention = sum_by_axis(
        jnp.dot(flat_values, out_proj, preferred_element_type=jnp.float32),
        (("dev_0", "dev_1", "dev_2"), "dev_3"),
        0,
    )
    stream = residual.astype(jnp.float32) + attention
    normed = (
        stream * lax.rsqrt(jnp.mean(stream * stream, axis=1, keepdims=True) + 1e-06) * norm_gain
    ).astype(jnp.bfloat16)
    group_count = lax.axis_size("group")
    dev_count = lax.axis_size(DEV)
    experts = dev_count // 2
    top_count = expert_ids.shape[1]
    capacity = max(tok_rows // 2, tok_rows * top_count // experts)
    flat_ids = expert_ids.reshape(-1)
    one_hot = (flat_ids[:, None] == jnp.arange(experts, dtype=jnp.int32)[None, :]).astype(jnp.int32)
    earlier = jnp.cumsum(one_hot, axis=0) - one_hot
    position = jnp.sum(earlier * one_hot, axis=1)
    slot_index = flat_ids * capacity + position
    slot_table = (
        jnp.arange(experts * capacity, dtype=jnp.int32)[:, None] == slot_index[None, :]
    ).astype(jnp.bfloat16)
    route_token = jnp.arange(tok_rows * top_count, dtype=jnp.int32) // top_count
    token_table = (route_token[:, None] == jnp.arange(tok_rows, dtype=jnp.int32)[None, :]).astype(
        jnp.bfloat16
    )
    placing = jnp.dot(slot_table, token_table, preferred_element_type=jnp.float32).astype(
        jnp.bfloat16
    )
    buffer = jnp.dot(placing, normed, preferred_element_type=jnp.float32).astype(jnp.bfloat16)
    paired = jnp.repeat(buffer.reshape(experts, capacity, feature_width), 2, axis=0)
    outgoing = jnp.tile(paired, (group_count, 1, 1))
    incoming = lax.all_to_all(outgoing, GROUP_DEV, split_axis=0, concat_axis=0, tiled=True)
    partial_value = expert_rows(incoming.reshape(-1, feature_width), w_gate, w_up, w_down).reshape(
        incoming.shape
    )
    returned = lax.all_to_all(
        partial_value.astype(jnp.bfloat16), GROUP_DEV, split_axis=0, concat_axis=0, tiled=True
    ).astype(partial_value.dtype)
    summed = returned.reshape(group_count, experts, 2, capacity, feature_width).sum(axis=(0, 2))
    picked = jnp.take(summed.reshape(experts * capacity, feature_width), slot_index, axis=0)
    picked = picked.reshape(tok_rows, top_count, feature_width)
    mixture = jnp.sum(picked * gate_values[:, :, None], axis=1)
    return (stream + mixture).astype(jnp.bfloat16)


def solution(mesh):
    finer = Mesh(
        mesh.devices.reshape(mesh.shape["group"], 4, 2, 4, 2),
        ("group", "dev_0", "dev_1", "dev_2", "dev_3"),
    )
    return jax.shard_map(
        local,
        mesh=finer,
        in_specs=(
            P(GROUP_DEV, None, None),
            P(GROUP_DEV, None, None),
            P(GROUP_DEV, None, None),
            P(GROUP_DEV, None, None),
            P(GROUP_DEV),
            P(DEV, None, None),
            P(DEV, None),
            P(GROUP_DEV, None),
            P(),
            P(GROUP_DEV, None),
            P(GROUP_DEV, None),
            P(DEV, None, "group"),
            P(DEV, None, "group"),
            P(DEV, "group", None),
        ),
        out_specs=P(GROUP_DEV, None),
        check_vma=False,
    )
```

profile of v0, /device:TPU:1, one launch (start us, length us, event | category | flops | bytes accessed | tf_op | source)
XLA Modules:
  0.0 281.9 jit_solution(11673829848724920338)
XLA Ops:
  0.0 0.0 copy-start
  0.0 0.0 copy-start.4
  0.0 0.0 copy-start.10
  0.0 1.2 copy-done
  1.2 1.6 fusion.31
  2.8 0.0 copy-done.4
  2.8 0.0 copy-done.10
  2.8 6.3 %multiply_select_fusion = f32[4,128,2048]{2,1,0:T(8,128)S(1)} fusion(f32[4,128,2048]{2,1,0:T(8,128)S(1)} %fusion.31, bf16[4,128,512]{2,1,0:T(8,128)(2,1)S(1)} %copy-done.4, bf16[4,2048,512]{2,1,0:T(8,128)(2,1)} %param.16, s32[4]{0:T(128)S(1)} %copy-done.10), kind=kOutput, calls=%fused_computation.8 | convolution fusion | flops 1077936128 | bytes 17301520 | tf_op jit(solution)/shard_map/thl,tcl->thc/dot_general | solution.py:33
  9.2 0.0 copy-start.2
  9.2 1.9 copy-done.2
  11.1 0.8 fusion.30
  11.9 7.6 %fusion.9 = bf16[4,128,512]{2,1,0:T(8,128)(2,1)S(1)} fusion(bf16[4,2048,512]{2,1,0:T(8,128)(2,1)} %param.16, f32[4,128]{1,0:T(4,128)S(1)} %fusion.30, f32[4,128,2048]{2,1,0:T(8,128)} %copy-done.2), kind=kOutput, calls=%fused_computation.18 | convolution fusion | flops 1077152256 | bytes 13109248 | tf_op jit(solution)/shard_map/thc,tcl->thl/dot_general | solution.py:45
  19.5 0.0 copy-start.6
  19.5 0.4 copy.29
  19.9 23.2 %all_to_all.38 = bf16[4,128,512]{2,0,1:T(4,128)(2,1)S(1)} all-to-all(bf16[4,128,512]{2,0,1:T(4,128)(2,1)S(1)} %copy.29), channel_id=1, replica_groups=mesh['group'=2,'dev_0'=4,'dev_1'=2,'dev_2'=4,'dev_3'=2] {'dev_0','dev_1'..., dimensions={1} | all-to-all | bytes 1048576 | tf_op jit(solution)/shard_map/all_to_all | solution.py:76
  43.1 0.2 copy.45
  43.3 0.1 all_to_all.28
  43.4 0.0 copy-done.6
  43.4 0.3 fusion.16
  43.7 0.1 copy.31
  43.9 0.1 dot_general.38
  44.0 3.2 %convolution_bitcast_fusion = f32[2,32,4,7168]{3,1,2,0:T(8,128)S(1)} fusion(bf16[256,7168]{1,0:T(8,128)(2,1)} %param.20, bf16[32,2,4,256]{3,2,1,0:T(4,128)(2,1)S(1)} %dot_general.38), kind=kOutput, calls=%fused_computation.2 | convolution fusion | flops 939524096 | bytes 11141120 | tf_op jit(solution)/shard_map/dot_general | solution.py:82
  47.1 10.9 %all_to_all.39 = f32[2,32,4,7168]{3,1,2,0:T(8,128)} all-to-all(f32[2,32,4,7168]{3,1,2,0:T(8,128)S(1)} %convolution_bitcast_fusion), channel_id=1, replica_groups=mesh['group'=2,'dev_0'=4,'dev_1'=2,'dev_2'=4,'dev_3'=2] {'dev_3'}, dimensions={0} | all-to-all | bytes 14680064 | tf_op jit(solution)/shard_map/all_to_all | solution.py:22
  58.0 5.9 %reduce_sum.68 = f32[32,4,7168]{2,0,1:T(8,128)} reduce(f32[2,32,4,7168]{3,1,2,0:T(8,128)} %all_to_all.39, f32[]{:T(128)} %constant.41.clone.1), dimensions={0}, to_apply=%region_2.3 | reduce | flops 917504 | bytes 11010052 | tf_op jit(solution)/shard_map/reduce_sum | solution.py:23
  63.9 6.2 %copy.33 = f32[32,4,7168]{2,1,0:T(4,128)} copy(f32[32,4,7168]{2,0,1:T(8,128)} %reduce_sum.68) | data formatting | bytes 7340032 | tf_op jit(solution)/shard_map/reduce_sum | solution.py:23
  70.1 0.0 copy-start.8
  70.1 5.1 %all-to-all-start.2 = ((f32[32,4,7168]{2,1,0:T(4,128)}), f32[32,4,7168]{2,1,0:T(4,128)}, u32[]{:S(2)}, u32[]{:S(2)}) async-start(f32[32,4,7168]{2,1,0:T(4,128)} %copy.33), calls=%async_computation.2 | async-start | bytes 7340032 | tf_op jit(solution)/shard_map/all_to_all | solution.py:29
  75.2 0.0 copy-done.8
  75.2 0.0 copy-start.5
  75.3 0.0 copy-start.7
  75.3 0.1 reshape.104
  75.3 0.1 fusion.25
  75.4 0.1 reduce_window_sum.11
  75.5 0.2 select_reduce_fusion
  75.7 48.2 %all-to-all-done.2 = f32[32,4,7168]{2,1,0:T(4,128)} async-done(((f32[32,4,7168]{2,1,0:T(4,128)}), f32[32,4,7168]{2,1,0:T(4,128)}, u32[]{:S(2)}, u32[]{:S(2)}) %all-to-all-start.2) | async-done | bytes 3670048 | tf_op jit(solution)/shard_map/all_to_all | solution.py:29
  123.8 2.6 reduce_sum.69
  126.5 0.0 copy-done.5
  126.5 0.2 multiply_reduce_fusion
  126.7 0.0 copy-done.7
  126.7 0.7 convolution_convert_fusion.1
  127.4 1.3 reshape.105
  128.7 2.1 broadcast_in_dim.15
  130.8 3.7 %tile.11 = bf16[2,64,2,7168]{3,2,1,0:T(2,128)(2,1)} broadcast(bf16[64,2,7168]{2,1,0:T(2,128)(2,1)S(1)} %bitcast.57), dimensions={1,2,3} | broadcast | bytes 5505024 | tf_op jit(solution)/shard_map/tile | solution.py:112
  134.5 56.6 %all_to_all.40 = bf16[128,2,7168]{2,1,0:T(2,128)(2,1)} all-to-all(bf16[128,2,7168]{2,1,0:T(2,128)(2,1)} %bitcast.56), channel_id=1, replica_groups=mesh['group'=2,'dev_0'=4,'dev_1'=2,'dev_2'=4,'dev_3'=2] {'group','dev_0'..., dimensions={0} | all-to-all | bytes 7340032 | tf_op jit(solution)/shard_map/all_to_all | solution.py:113
  191.1 8.4 %reshape.106 = bf16[256,7168]{1,0:T(8,128)(2,1)} reshape(bf16[128,2,7168]{2,1,0:T(2,128)(2,1)} %all_to_all.40) | data formatting | bytes 7340032 | tf_op jit(solution)/shard_map/reshape | solution.py:114
  199.5 4.4 %fusion.5 = f32[256,256]{1,0:T(8,128)S(1)} fusion(bf16[256,7168]{1,0:T(8,128)(2,1)} %reshape.106, bf16[1,7168,256]{2,1,0:T(8,128)(2,1)} %param.25), kind=kOutput, calls=%fused_computation.14 | convolution fusion | flops 939524096 | bytes 7602176 | tf_op jit(solution)/shard_map/dot_general | solution.py:51
  204.0 0.0 copy-done.3
  204.0 0.9 copy-done.11
  204.8 1.1 fusion.13
  206.0 0.1 dot_general.44
  206.0 3.2 %convolution_convert_fusion = bf16[128,2,7168]{2,0,1:T(8,128)(2,1)S(1)} fusion(bf16[1,256,7168]{2,1,0:T(8,128)(2,1)} %param.27, bf16[128,2,256]{2,1,0:T(2,128)(2,1)S(1)} %dot_general.44), kind=kOutput, calls=%fused_computation.3 | convolution fusion | flops 941359104 | bytes 7471104 | tf_op jit(solution)/shard_map/dot_general | solution.py:54
  209.2 5.6 %copy.35 = bf16[128,2,7168]{2,1,0:T(2,128)(2,1)} copy(bf16[128,2,7168]{2,0,1:T(8,128)(2,1)S(1)} %convolution_convert_fusion) | data formatting | bytes 7340032 | tf_op jit(solution)/shard_map/convert_element_type | solution.py:118
  214.8 5.6 %all-to-all-start.4 = ((bf16[128,2,7168]{2,1,0:T(2,128)(2,1)}), bf16[128,2,7168]{2,1,0:T(2,128)(2,1)}, u32[]{:S(2)}, u32[]{:S(2)}) async-start(bf16[128,2,7168]{2,1,0:T(2,128)(2,1)} %copy.35), calls=%async_computation.4 | async-start | bytes 7340032 | tf_op jit(solution)/shard_map/all_to_all | solution.py:117
  220.4 0.1 reduce_sum.71
  220.5 0.1 mul.84
  220.6 46.9 %all-to-all-done.4 = bf16[128,2,7168]{2,1,0:T(2,128)(2,1)} async-done(((bf16[128,2,7168]{2,1,0:T(2,128)(2,1)}), bf16[128,2,7168]{2,1,0:T(2,128)(2,1)}, u32[]{:S(2)}, u32[]{:S(2)}) %all-to-all-start.4) | async-done | bytes 3670048 | tf_op jit(solution)/shard_map/all_to_all | solution.py:117
  267.5 7.8 %convert_reduce_fusion = f32[32,2,7168]{2,1,0:T(2,128)} fusion(bf16[2,32,2,2,7168]{4,3,2,1,0:T(2,128)(2,1)} %bitcast.17), kind=kLoop, calls=%fused_computation.5 | loop fusion | flops 3211264 | bytes 5505024 | tf_op jit(solution)/shard_map/reduce_sum | solution.py:120
  275.3 2.7 reshape.109
  278.0 0.0 copy-start.9
  278.0 1.7 gather_fusion
  279.7 0.0 copy-done.9
  279.7 1.5 fusion.18
  281.3 0.7 add_convert_fusion
  281.9 0.0 copy-done.1
  (9 shorter events, 0.0 us)
Async XLA Ops:
  0.0 1.2 copy-start
  0.0 2.8 copy-start.4
  0.0 2.8 copy-start.10
  9.2 1.9 copy-start.2
  19.5 23.9 %copy-start.6 = (bf16[2,512,128]{2,1,0:T(8,128)(2,1)S(1)}, bf16[2,512,128]{2,1,0:T(8,128)(2,1)}, u32[]{:S(2)}) copy-start(bf16[2,512,128]{2,1,0:T(8,128)(2,1)} %param.19) | copy-start | bytes 786436
  70.1 5.1 %copy-start.8 = (s32[4,8]{1,0:T(4,128)S(1)}, s32[4,8]{1,0:T(4,128)}, u32[]{:S(2)}) copy-start(s32[4,8]{1,0:T(4,128)} %param.23) | copy-start | bytes 388
  70.1 53.8 %all-to-all-start.2 = ((f32[32,4,7168]{2,1,0:T(4,128)}), f32[32,4,7168]{2,1,0:T(4,128)}, u32[]{:S(2)}, u32[]{:S(2)}) async-start(f32[32,4,7168]{2,1,0:T(4,128)} %copy.33), calls=%async_computation.2 | async-start | bytes 7340032 | tf_op jit(solution)/shard_map/all_to_all | solution.py:29
  75.2 51.2 %copy-start.5 = (bf16[4,7168]{1,0:T(4,128)(2,1)S(1)}, bf16[4,7168]{1,0:T(4,128)(2,1)}, u32[]{:S(2)}) copy-start(bf16[4,7168]{1,0:T(4,128)(2,1)} %param.21) | copy-start | bytes 172036
  75.3 51.4 %copy-start.7 = (f32[7168]{0:T(1024)S(1)}, f32[7168]{0:T(1024)}, u32[]{:S(2)}) copy-start(f32[7168]{0:T(1024)} %param.22) | copy-start | bytes 86020
  199.5 4.4 %copy-start.3 = (bf16[256,7168]{1,0:T(8,128)(2,1)S(1)}, bf16[256,7168]{1,0:T(8,128)(2,1)}, u32[]{:S(2)}) copy-start(bf16[256,7168]{1,0:T(8,128)(2,1)} %reshape.106) | copy-start | bytes 11010052
  199.5 5.3 %copy-start.11 = (bf16[1,7168,256]{2,1,0:T(8,128)(2,1)S(1)}, bf16[1,7168,256]{2,1,0:T(8,128)(2,1)}, u32[]{:S(2)}) copy-start(bf16[1,7168,256]{2,1,0:T(8,128)(2,1)} %param.26) | copy-start | bytes 11010052
  214.8 52.7 %all-to-all-start.4 = ((bf16[128,2,7168]{2,1,0:T(2,128)(2,1)}), bf16[128,2,7168]{2,1,0:T(2,128)(2,1)}, u32[]{:S(2)}, u32[]{:S(2)}) async-start(bf16[128,2,7168]{2,1,0:T(2,128)(2,1)} %copy.35), calls=%async_computation.4 | async-start | bytes 7340032 | tf_op jit(solution)/shard_map/all_to_all | solution.py:117
  275.3 6.7 %copy-start.1 = (bf16[4,64,2048]{2,1,0:T(8,128)(2,1)S(1)}, bf16[4,64,2048]{2,1,0:T(8,128)(2,1)}, u32[]{:S(2)}) copy-start(bf16[4,64,2048]{2,1,0:T(8,128)(2,1)} %param.17) | copy-start | bytes 3145732
  278.0 1.8 copy-start.9
where the time goes:
time: 283 us; the launch traced here: 282 us
  waiting for transfers between devices  95.1 us (34%)
  blocking collectives  90.7 us (32%)
  local copies, waits for them, and re-layouts  37 us (13%)
  matrix products  28.3 us (10%)
  other arithmetic  19.8 us (7%)
  starting transfers between devices  10.7 us (4%)
    all_to_all x1, blocking collectives, local(): lax.all_to_all(outgoing, GROUP_DEV, split_axis=0, concat_axis=0, tiled=True)  56.6 us
    all_to_all x1, waiting for transfers between devices, sum_by_axis(): return jnp.sum(lax.all_to_all(own, far, 0, 0, tiled=True), axis=0)  48.2 us
    all_to_all x1, waiting for transfers between devices, local(): lax.all_to_all(partial_value.astype(jnp.bfloat16), GROUP_DEV, split_axis=...  46.9 us
    all_to_all x1, blocking collectives, local(): lax.all_to_all(mixed_latent, DEV, split_axis=1, concat_axis=0, tiled=True)  23.2 us
    all_to_all x1, blocking collectives, sent_and_summed(): tiles = lax.all_to_all(split_up(array, dim, size), axis, 0, 0, tiled=True)  10.9 us
    reshape x1, local copies, waits for them, and re-layouts, local(): incoming.reshape(-1, feature_width)  8.4 us
    reduce_sum x1, other arithmetic, local(): returned.reshape(group_count, experts, 2, capacity, feature_width)  7.75 us
    dot_general x1, matrix products, attend(): jnp.einsum('thc,tcl->thl', attn_weights, cache_latent, preferred_element_...  7.61 us
  transfers between devices with their start and end apart: 2, of which 2 were waited for; matrix products, arithmetic and copies ran while one was open for 0% of the time, Pallas kernels for 0%

commit v1 on v0

v1 whole, which is shorter than its diff:
```python
import jax
import jax.numpy as jnp
from jax import lax
from jax.sharding import Mesh
from jax.sharding import PartitionSpec as P

DEV = ("dev_0", "dev_1", "dev_2", "dev_3")
GROUP_DEV = ("group", "dev_0", "dev_1", "dev_2", "dev_3")


softmax_scale = 192.0 ** (-0.5)


def attend(query_latent, query_rope, cache_latent, cache_rope, lengths):
    scores = jnp.einsum(
        "thl,tcl->thc", query_latent, cache_latent, preferred_element_type=jnp.float32
    )
    scores = scores + jnp.einsum(
        "thr,trc->thc", query_rope, cache_rope, preferred_element_type=jnp.float32
    )
    scores = scores * softmax_scale
    positions = lax.broadcasted_iota(jnp.int32, scores.shape, 2)
    scores = jnp.where(positions < lengths[:, None, None], scores, -jnp.inf)
    row_peak = jnp.max(scores, axis=2, keepdims=True)
    weights = jnp.exp(scores - row_peak)
    attn_weights = (weights / jnp.sum(weights, axis=2, keepdims=True)).astype(jnp.bfloat16)
    return jnp.einsum(
        "thc,tcl->thl", attn_weights, cache_latent, preferred_element_type=jnp.float32
    ).astype(jnp.bfloat16)


def expert_rows(token_rows, w_gate, w_up, w_down):
    gate_part = jnp.dot(token_rows, w_gate[0], preferred_element_type=jnp.float32)
    up_part = jnp.dot(token_rows, w_up[0], preferred_element_type=jnp.float32)
    active = (jax.nn.silu(gate_part) * up_part).astype(jnp.bfloat16)
    return jnp.dot(active, w_down[0], preferred_element_type=jnp.float32)


def local(
    query_latent,
    query_rope,
    cache_latent,
    cache_rope,
    lengths,
    value_up,
    out_proj,
    residual,
    norm_gain,
    expert_ids,
    gate_values,
    w_gate,
    w_up,
    w_down,
):
    tok_rows = query_latent.shape[0]
    feature_width = residual.shape[1]
    mixed_latent = attend(query_latent, query_rope, cache_latent, cache_rope, lengths)
    by_head = lax.all_to_all(mixed_latent, DEV, split_axis=1, concat_axis=0, tiled=True)
    head_values = jnp.einsum(
        "thl,hlv->thv", by_head, value_up, preferred_element_type=jnp.float32
    ).astype(jnp.bfloat16)
    flat_values = head_values.reshape(head_values.shape[0], -1)
    attention_part = jnp.dot(flat_values, out_proj, preferred_element_type=jnp.float32)
    attention = lax.psum_scatter(
        attention_part.astype(jnp.bfloat16), DEV, scatter_dimension=0, tiled=True
    ).astype(jnp.float32)
    stream = residual.astype(jnp.float32) + attention
    normed = (
        stream * lax.rsqrt(jnp.mean(stream * stream, axis=1, keepdims=True) + 1e-06) * norm_gain
    ).astype(jnp.bfloat16)
    experts = lax.axis_size(DEV) // 2
    expert_range = jnp.arange(experts, dtype=jnp.int32)
    chosen = expert_ids[:, :, None] == expert_range[None, None, :]
    row_gates = jnp.sum(jnp.where(chosen, gate_values[:, :, None], 0.0), axis=1)
    all_rows = lax.all_gather(normed, GROUP_DEV, axis=0, tiled=True)
    all_gates = lax.all_gather(row_gates, GROUP_DEV, axis=0, tiled=True)
    mine = lax.axis_index(DEV) // 2
    my_gates = jnp.sum(jnp.where(expert_range[None, :] == mine, all_gates, 0.0), axis=1)
    partial_value = expert_rows(all_rows, w_gate, w_up, w_down) * my_gates[:, None]
    mixture = lax.psum_scatter(
        partial_value.astype(jnp.bfloat16), GROUP_DEV, scatter_dimension=0, tiled=True
    ).astype(jnp.float32)
    return (stream + mixture).astype(jnp.bfloat16)


def solution(mesh):
    finer = Mesh(
        mesh.devices.reshape(mesh.shape["group"], 4, 2, 4, 2),
        ("group", "dev_0", "dev_1", "dev_2", "dev_3"),
    )
    return jax.shard_map(
        local,
        mesh=finer,
        in_specs=(
            P(GROUP_DEV, None, None),
            P(GROUP_DEV, None, None),
            P(GROUP_DEV, None, None),
            P(GROUP_DEV, None, None),
            P(GROUP_DEV),
            P(DEV, None, None),
            P(DEV, None),
            P(GROUP_DEV, None),
            P(),
            P(GROUP_DEV, None),
            P(GROUP_DEV, None),
            P(DEV, None, "group"),
            P(DEV, None, "group"),
            P(DEV, "group", None),
        ),
        out_specs=P(GROUP_DEV, None),
        check_vma=False,
    )
```

time: 283 us -> 1020 us (3.60)
  waiting for transfers between devices: 95.1 us -> 739 us
  blocking collectives: 90.7 us -> 201 us
  local copies, waits for them, and re-layouts: 37 us -> 16.6 us
  matrix products: 28.3 us -> 43.1 us
  other arithmetic: 19.8 us -> 5.41 us
  between operations: 0.26 us -> 14 us
  starting transfers between devices: 10.7 us -> 0.09 us
    unnamed x0 -> x5, waiting for transfers between devices: none -> 716 us
    all_gather x0 -> x1, blocking collectives: none -> 178 us  [local(): all_gates = lax.all_gather(row_gates, GROUP_DEV, axis=0, tiled=True)]
    all_to_all x2 -> x0, waiting for transfers between devices: 95.1 us -> none  [the longest x1 48.2 us: sum_by_axis(): return jnp.sum(lax.all_to_all(own, far, 0, 0, tiled=True), axis=0)]
    all_to_all x2 -> x0, blocking collectives: 67.5 us -> none  [the longest x1 56.6 us: local(): lax.all_to_all(outgoing, GROUP_DEV, split_axis=0, concat_axis=0, tiled=True)]
    all_gather x0 -> x1, waiting for transfers between devices: none -> 23.3 us  [local(): all_rows = lax.all_gather(normed, GROUP_DEV, axis=0, tiled=True)]
    reduce_sum x5 -> x2, other arithmetic: 18 us -> 0.24 us  [the longest x1 0.14 us: local(): jnp.sum(jnp.where(expert_range[None, :] == mine, all_gates, 0.0), axis=1)]
    dot_general x1, matrix products: 3.16 us -> 16.1 us  [expert_rows(): return jnp.dot(active, w_down[0], preferred_element_type=jnp.float32)]
    reshape x4 -> x0, local copies, waits for them, and re-layouts: 12.4 us -> none  [the longest x1 8.4 us: local(): incoming.reshape(-1, feature_width)]
  transfers between devices with their start and end apart: 2 -> 3, of which waited for: 2 -> 3; matrix products, arithmetic and copies ran while one was open for 0% -> 0% of each run, Pallas kernels for 0% -> 0%
where the time goes in v1:
time: 1020 us
  waiting for transfers between devices  739 us (72%)
  blocking collectives  201 us (20%)
  matrix products  43.1 us (4%)
  local copies, waits for them, and re-layouts  16.6 us (2%)
  between operations  14 us (1%)
    unnamed x5, waiting for transfers between devices  716 us
    all_gather x1, blocking collectives, local(): all_gates = lax.all_gather(row_gates, GROUP_DEV, axis=0, tiled=True)  178 us
    all_gather x1, waiting for transfers between devices, local(): all_rows = lax.all_gather(normed, GROUP_DEV, axis=0, tiled=True)  23.3 us
    all_to_all x1, blocking collectives, local(): lax.all_to_all(mixed_latent, DEV, split_axis=1, concat_axis=0, tiled=True)  23.2 us
  transfers between devices with their start and end apart: 3, of which 3 were waited for; matrix products, arithmetic and copies ran while one was open for 0% of the time, Pallas kernels for 0%

profile of v1, /device:TPU:1, one launch (start us, length us, event | category | flops | bytes accessed | tf_op | source)
XLA Modules:
  0.0 1019.2 jit_solution(3751967246180345959)
XLA Ops:
  6.5 0.0 copy-start
  6.5 0.0 copy-start.9
  6.5 0.0 copy-start.3
  6.5 0.0 all-reduce.5.cloned.1.call-start
  6.5 1.2 copy-done
  7.8 1.6 fusion.22
  9.3 0.0 copy-done.9
  9.4 0.0 copy-done.3
  9.4 6.3 multiply_select_fusion
  15.7 0.0 copy-start.2
  15.7 1.9 copy-done.2
  17.6 0.8 fusion.21
  18.4 7.6 fusion.8
  26.0 0.0 copy-start.5
  26.0 0.4 copy.20
  26.4 23.2 %all_to_all.18 = bf16[4,128,512]{2,0,1:T(4,128)(2,1)S(1)} all-to-all(bf16[4,128,512]{2,0,1:T(4,128)(2,1)S(1)} %copy.20), channel_id=1, replica_groups=mesh['group'=2,'dev_0'=4,'dev_1'=2,'dev_2'=4,'dev_3'=2] {'dev_0','dev_1'..., dimensions={1} | all-to-all | bytes 1048576 | tf_op jit(solution)/shard_map/all_to_all | solution.py:58
  49.6 0.2 copy.25
  49.8 0.1 all_to_all.16
  49.9 0.0 copy-done.5
  49.9 0.3 convolution_convert_fusion.1
  50.3 0.0 copy-start.10
  50.3 0.0 copy-start.4
  50.3 0.0 copy-start.6
  50.3 0.0 copy-start.7
  50.3 0.0 copy-start.8
  50.3 5.0 convolution_convert_fusion
  55.3 0.0 all-reduce.5.cloned.1.call-update
  55.4 0.0 all-gather.4.cloned.1.call-start
  55.4 0.0 copy-done.10
  55.4 0.6 dynamic-slice
  56.7 557.5 %all-reduce.5.cloned.1.call-done = bf16[256,7168]{1,0:T(8,128)(2,1)} async-done(((bf16[256,7168]{1,0:T(8,128)(2,1)}), bf16[256,7168]{1,0:T(8,128)(2,1)}) %all-reduce.5.cloned.1.call-update) | async-done | bytes 3670032
  614.1 0.0 copy-done.4
  614.1 1.1 multiply_reduce_fusion
  615.2 0.0 copy-done.6
  615.2 1.6 fusion.18
  616.8 0.0 all-gather.4.cloned.1.call-update
  616.9 0.0 all-reduce.7.cloned.1.call-start
  616.9 0.0 copy-done.7
  616.9 0.0 copy-done.8
  616.9 0.1 select_reduce_fusion.1
  617.0 177.6 %all-gather.1 = f32[128,4,32]{2,1,0:T(4,128)S(1)} all-gather(f32[1,4,32]{2,1,0:T(4,128)S(1)} %bitcast.46), channel_id=1, replica_groups=mesh['group'=2,'dev_0'=4,'dev_1'=2,'dev_2'=4,'dev_3'=2] {'group','dev_0'..., dimensions={0}, use_global_device_ids=true | all-gather | bytes 66048 | tf_op jit(solution)/shard_map/all_gather | solution.py:76
  794.6 0.1 select_reduce_fusion
  794.8 23.3 %all-gather.4.cloned.1.call-done = bf16[128,4,7168]{2,1,0:T(4,128)(2,1)} async-done(((bf16[1,4,7168]{2,1,0:T(4,128)(2,1)}), bf16[128,4,7168]{2,1,0:T(4,128)(2,1)}) %all-gather.4.cloned.1.call-update) | async-done | bytes 7340048 | tf_op jit(solution)/shard_map/all_gather | solution.py:75
  818.1 12.1 %reshape.25 = bf16[512,7168]{1,0:T(8,128)(2,1)} reshape(bf16[128,4,7168]{2,1,0:T(4,128)(2,1)} %all-gather.4.cloned.1.call-done) | data formatting | bytes 14680064
  830.2 6.2 fusion.4
  836.4 0.0 copy-start.1
  836.4 16.1 %multiply_convert_fusion = bf16[512,7168]{1,0:T(8,128)(2,1)} fusion(f32[512]{0:T(512)S(1)} %select_reduce_fusion, bf16[1,256,7168]{2,1,0:T(8,128)(2,1)} %param.27, bf16[512,7168]{1,0:T(8,128)(2,1)} %reshape.25, bf16[1,7168,256]{2,1,0:T(8,128)(2,1)} %param.26, f32[512,256]{1,0:T(8,128)S(1)} %fusion.4), kind=kOutput, calls=%fused_computation.1 | convolution fusion | flops 3766222848 | bytes 22546432 | tf_op jit(solution)/shard_map/dot_general | solution.py:36
  852.5 0.0 all-reduce.7.cloned.1.call-update
  852.5 158.5 %all-reduce.7.cloned.1.call-done = bf16[512,7168]{1,0:T(8,128)(2,1)} async-done(((bf16[512,7168]{1,0:T(8,128)(2,1)}), bf16[512,7168]{1,0:T(8,128)(2,1)}) %all-reduce.7.cloned.1.call-update) | async-done | bytes 7340048
  1011.1 1.7 add_convert_fusion
  1012.7 0.0 copy-done.1
  (2 shorter events, 0.0 us)
Async XLA Ops:
  6.5 1.2 copy-start
  6.5 2.8 copy-start.9
  6.5 2.8 copy-start.3
  6.5 607.6 %all-reduce.5.cloned.1.call-start = ((), (), s32[]{:S(2)}) async-start(), calls=%async_computation.2 | async-start | bytes 7340032
  15.7 1.9 copy-start.2
  26.0 23.9 %copy-start.5 = (bf16[2,512,128]{2,1,0:T(8,128)(2,1)S(1)}, bf16[2,512,128]{2,1,0:T(8,128)(2,1)}, u32[]{:S(2)}) copy-start(bf16[2,512,128]{2,1,0:T(8,128)(2,1)} %param.19) | copy-start | bytes 786436
  50.3 5.2 copy-start.10
  50.3 563.8 %copy-start.4 = (bf16[4,7168]{1,0:T(4,128)(2,1)S(1)}, bf16[4,7168]{1,0:T(4,128)(2,1)}, u32[]{:S(2)}) copy-start(bf16[4,7168]{1,0:T(4,128)(2,1)} %param.21) | copy-start | bytes 172036
  50.3 564.9 %copy-start.6 = (f32[7168]{0:T(1024)S(1)}, f32[7168]{0:T(1024)}, u32[]{:S(2)}) copy-start(f32[7168]{0:T(1024)} %param.22) | copy-start | bytes 86020
  50.3 566.6 %copy-start.7 = (f32[4,8]{1,0:T(4,128)S(1)}, f32[4,8]{1,0:T(4,128)}, u32[]{:S(2)}) copy-start(f32[4,8]{1,0:T(4,128)} %param.24) | copy-start | bytes 388
  50.3 566.6 %copy-start.8 = (s32[4,8]{1,0:T(4,128)S(1)}, s32[4,8]{1,0:T(4,128)}, u32[]{:S(2)}) copy-start(s32[4,8]{1,0:T(4,128)} %param.23) | copy-start | bytes 388
  55.4 762.8 %all-gather.4.cloned.1.call-start = ((), (), s32[]{:S(2)}) async-start(), calls=%async_computation.1 | async-start | bytes 7397376 | tf_op jit(solution)/shard_map/all_gather | solution.py:75
  616.9 394.2 %all-reduce.7.cloned.1.call-start = ((), (), s32[]{:S(2)}) async-start(), calls=%async_computation.3 | async-start | bytes 14680064
  836.4 176.3 %copy-start.1 = (bf16[4,64,2048]{2,1,0:T(8,128)(2,1)S(1)}, bf16[4,64,2048]{2,1,0:T(8,128)(2,1)}, u32[]{:S(2)}) copy-start(bf16[4,64,2048]{2,1,0:T(8,128)(2,1)} %param.17) | copy-start | bytes 3145732
Sparse Core Ops, SparseCore 0:
  55.5 558.5 all-reduce.4
  617.0 201.1 all-gather.3
  852.7 158.3 all-reduce.6

commit v2 on v1

v2 whole, which is shorter than its diff:
```python
import functools

import jax
import jax.numpy as jnp
from jax import lax
from jax.experimental import pallas as pl
from jax.experimental.pallas import tpu as pltpu
from jax.sharding import Mesh
from jax.sharding import PartitionSpec as P

DEV = ("dev_0", "dev_1", "dev_2", "dev_3")
GROUP_DEV = ("group", "dev_0", "dev_1", "dev_2", "dev_3")
MESH = pl.DeviceIdType.MESH


softmax_scale = 192.0 ** (-0.5)


def attend(query_latent, query_rope, cache_latent, cache_rope, lengths):
    scores = jnp.einsum(
        "thl,tcl->thc", query_latent, cache_latent, preferred_element_type=jnp.float32
    )
    scores = scores + jnp.einsum(
        "thr,trc->thc", query_rope, cache_rope, preferred_element_type=jnp.float32
    )
    scores = scores * softmax_scale
    positions = lax.broadcasted_iota(jnp.int32, scores.shape, 2)
    scores = jnp.where(positions < lengths[:, None, None], scores, -jnp.inf)
    row_peak = jnp.max(scores, axis=2, keepdims=True)
    weights = jnp.exp(scores - row_peak)
    attn_weights = (weights / jnp.sum(weights, axis=2, keepdims=True)).astype(jnp.bfloat16)
    return jnp.einsum(
        "thc,tcl->thl", attn_weights, cache_latent, preferred_element_type=jnp.float32
    ).astype(jnp.bfloat16)


HALF = 3584
UNIT = 256
ATTN_COLS = (((0, 1024), (1024, 768)), ((1792, 1024), (2816, 768)))
ATTN_ORDERS = (("z", "y"), ("y", "z"))
GATHER_COLS = (((0, 640), (640, 640)), ((1280, 640), (1920, 640)), ((2560, 640), (3200, 512)))
MIX_COLS = (((0, 768), (768, 512)), ((1280, 768), (2048, 512)), ((2560, 512), (3072, 512)))
ORDERS = (("z", "y", "x"), ("y", "x", "z"), ("x", "z", "y"))


def tail_kernel(
    values_ref,
    residual_ref,
    gain_ref,
    gates_ref,
    proj_hbm,
    gate_hbm,
    up_hbm,
    down_hbm,
    out_ref,
    proj,
    w_gate,
    w_up,
    w_down,
    attn_out,
    attn_in,
    attn_sum,
    attn_land0a,
    attn_land0b,
    attn_land1,
    attn_land2,
    attn_own,
    swap_out,
    swap_in,
    row_out,
    row_in,
    rows,
    gate_acc,
    up_acc,
    active,
    mix_out,
    mix_in,
    mix_sum,
    mix_land0,
    mix_land1,
    mix_land2,
    load_sem,
    send_sem,
    recv_sem,
):
    group = lax.axis_index("group")
    x_lo = lax.axis_index("dev_1")
    core = lax.axis_index("dev_3")
    pos = {"z": lax.axis_index("dev_0"), "y": lax.axis_index("dev_2"), "x": 2 * group + x_lo}
    other = 1 - core
    first_core = core == 0

    def above(dim):
        return lax.rem(pos[dim] + 1, 4)

    def below(dim):
        return lax.rem(pos[dim] + 3, 4)

    def across(dim):
        return lax.rem(pos[dim] + 2, 4)

    def device(dim, place):
        if dim == "z":
            return {"dev_0": place}
        if dim == "y":
            return {"dev_2": place}
        return {"group": lax.div(place, 2), "dev_1": lax.rem(place, 2)}

    partner = {"dev_3": other}
    x_pair = {"dev_1": 1 - x_lo}
    sent = []

    def send(src, dst, to):
        number = len(sent)
        copy = pltpu.make_async_remote_copy(
            src_ref=src,
            dst_ref=dst,
            send_sem=send_sem.at[number],
            recv_sem=recv_sem.at[number],
            device_id=to,
            device_id_type=MESH,
        )
        copy.start()
        sent.append(copy)
        return copy

    loads = []
    for number, (src, dst) in enumerate(
        ((proj_hbm, proj), (gate_hbm, w_gate), (up_hbm, w_up), (down_hbm, w_down))
    ):
        load = pltpu.make_async_copy(src, dst, load_sem.at[number])
        load.start()
        loads.append(load)

    barrier = pltpu.get_barrier_semaphore()
    pl.semaphore_signal(barrier, inc=1, device_id=partner, device_id_type=MESH)
    for dim in ("x", "y", "z"):
        for place in (above(dim), below(dim)):
            pl.semaphore_signal(barrier, inc=1, device_id=device(dim, place), device_id_type=MESH)
    pl.semaphore_wait(barrier, 7)

    def ring_start(dim, block, land, cols, part):
        first, second = cols
        up, down = device(dim, above(dim)), device(dim, below(dim))
        if part == 0:
            return (
                send(block(across(dim), first), land(0, first), up),
                send(block(below(dim), first), land(1, first), down),
            )
        return (
            send(block(across(dim), second), land(2, second), down),
            send(block(above(dim), second), land(3, second), up),
        )

    def add_into(target, *terms):
        total = target[...].astype(jnp.float32)
        for term in terms:
            total = total + term[...].astype(jnp.float32)
        return total

    def ring_relay(dim, block, land, cols, started):
        first, second = cols
        up, down = device(dim, above(dim)), device(dim, below(dim))
        started[0][0].wait_recv()
        target = block(above(dim), first)
        target[...] = add_into(target, land(0, first)).astype(jnp.bfloat16)
        upward = send(target, land(4, first), up)
        started[1][0].wait_recv()
        target = block(below(dim), second)
        target[...] = add_into(target, land(2, second)).astype(jnp.bfloat16)
        downward = send(target, land(5, second), down)
        return upward, downward

    def ring_finish(dim, block, land, cols, started, relayed, store):
        first, second = cols
        started[0][1].wait_recv()
        relayed[0].wait_recv()
        store(first, add_into(block(pos[dim], first), land(1, first), land(4, first)))
        started[1][1].wait_recv()
        relayed[1].wait_recv()
        store(second, add_into(block(pos[dim], second), land(3, second), land(5, second)))

    def span(cols):
        return pl.ds(cols[0], cols[1])

    def swap_halves(own):
        top, bottom = own[0:4, :], own[4:8, :]
        swap_out[...] = jnp.where(first_core, bottom, top)
        swapped = send(swap_out, swap_in.at[swap_count[0]], partner)
        swap_count[0] += 1
        swapped.wait_recv()
        mine = jnp.where(first_core, top, bottom)
        theirs = swap_in[swap_count[0] - 1]
        return jnp.where(first_core, mine, theirs), jnp.where(first_core, theirs, mine), swapped

    swap_count = [0]

    values = values_ref[...].reshape(256, 256)
    loads[0].wait()
    handed = {}

    def attn_units(cols, half, store):
        for start in range(cols[0], cols[0] + cols[1], UNIT):
            at = pl.multiple_of(half * HALF + start, 128)
            part = jnp.dot(
                values, proj[:, pl.ds(at, UNIT)], preferred_element_type=jnp.float32
            ).reshape(4, 2, 4, 8, UNIT)
            store(start, part)

    for rotation in range(2):
        for part in range(2):
            cols = ATTN_COLS[rotation][part]

            def store_out(start, value):
                attn_out[:, :, :, :, pl.ds(start, UNIT)] = value.astype(jnp.bfloat16)

            attn_units(cols, other, store_out)
            piece = (slice(None), slice(None), slice(None), slice(None), span(cols))
            handed[rotation, part] = send(attn_out.at[piece], attn_in.at[piece], partner)

    def attn_block(rotation, phase):
        dims = ATTN_ORDERS[rotation]

        def block(place, cols):
            at = {}
            for earlier in dims[:phase]:
                at[earlier] = pos[earlier]
            at[dims[phase]] = place
            return attn_sum.at[
                at.get("z", slice(None)), slice(None), at.get("y", slice(None)), slice(None), span(cols)
            ]

        return block

    def attn_land(rotation, phase):
        if phase == 0:
            land = (attn_land0a, attn_land0b)[rotation]
            return lambda slot, cols: land.at[
                slot, slice(None), slice(None), slice(None), pl.ds(0, cols[1])
            ]
        return lambda slot, cols: attn_land1.at[
            rotation, slot, slice(None), slice(None), pl.ds(0, cols[1])
        ]

    started = {}
    for rotation in range(2):
        dim = ATTN_ORDERS[rotation][0]
        for part in range(2):
            cols = ATTN_COLS[rotation][part]
            handed[rotation, part].wait_recv()

            def store_sum(start, value):
                at = (slice(None), slice(None), slice(None), slice(None), pl.ds(start, UNIT))
                total = value + attn_in[at].astype(jnp.float32)
                attn_sum[at] = total.astype(jnp.bfloat16)

            attn_units(cols, core, store_sum)
            started[rotation, part] = ring_start(
                dim, attn_block(rotation, 0), attn_land(rotation, 0), ATTN_COLS[rotation], part
            )
    paired = {}
    for phase in range(2):
        relayed = {}
        for rotation in range(2):
            relayed[rotation] = ring_relay(
                ATTN_ORDERS[rotation][phase],
                attn_block(rotation, phase),
                attn_land(rotation, phase),
                ATTN_COLS[rotation],
                (started[rotation, 0], started[rotation, 1]),
            )
        for rotation in range(2):
            dim = ATTN_ORDERS[rotation][phase]
            block = attn_block(rotation, phase)

            def store(cols, total):
                block(pos[dim], cols)[...] = total.astype(jnp.bfloat16)

            ring_finish(
                dim,
                block,
                attn_land(rotation, phase),
                ATTN_COLS[rotation],
                (started[rotation, 0], started[rotation, 1]),
                relayed[rotation],
                store,
            )
            if phase == 0:
                for part in range(2):
                    started[rotation, part] = ring_start(
                        ATTN_ORDERS[rotation][1],
                        attn_block(rotation, 1),
                        attn_land(rotation, 1),
                        ATTN_COLS[rotation],
                        part,
                    )
            else:
                width = ATTN_COLS[rotation][0][1] + ATTN_COLS[rotation][1][1]
                piece = pl.ds(ATTN_COLS[rotation][0][0], width)
                paired[rotation] = send(
                    attn_sum.at[pos["z"], 1 - x_lo, pos["y"], slice(None), piece],
                    attn_land2.at[slice(None), piece],
                    x_pair,
                )
    for rotation in range(2):
        paired[rotation].wait_recv()
    attn_own[...] = attn_sum[pos["z"], x_lo, pos["y"]].astype(jnp.float32) + attn_land2[
        ...
    ].astype(jnp.float32)
    low, high, swapped = swap_halves(attn_own)
    stream_low = residual_ref[:, 0:HALF].astype(jnp.float32) + low
    stream_high = residual_ref[:, HALF : 2 * HALF].astype(jnp.float32) + high
    square = jnp.sum(stream_low * stream_low, axis=1, keepdims=True) + jnp.sum(
        stream_high * stream_high, axis=1, keepdims=True
    )
    scale = lax.rsqrt(square / (2 * HALF) + 1e-06)
    dense = gates_ref[...]
    coarse = dense.astype(jnp.bfloat16).astype(jnp.float32)
    lane = lax.broadcasted_iota(jnp.int32, dense.shape, 1)
    packed = jnp.where(lane < 32, coarse, jnp.where(lane < 64, dense - coarse, 0.0))
    row_out[0, :, 0:HALF] = (stream_low * scale * gain_ref[:, 0:HALF]).astype(jnp.bfloat16)
    row_out[1, :, 0:HALF] = (stream_high * scale * gain_ref[:, HALF : 2 * HALF]).astype(
        jnp.bfloat16
    )
    row_out[0, :, HALF : HALF + 128] = packed.astype(jnp.bfloat16)
    row_out[1, :, HALF : HALF + 128] = packed.astype(jnp.bfloat16)
    handed_rows = send(row_out.at[other], row_in, partner)
    out_ref[:, 0:HALF] = stream_low
    out_ref[:, HALF : 2 * HALF] = stream_high

    handed_rows.wait_recv()
    mine = row_out[core].astype(jnp.float32)
    theirs = row_in[...].astype(jnp.float32)
    rows[core, pos["x"], pos["y"], pos["z"]] = jnp.concatenate(
        [jnp.where(first_core, mine, theirs), jnp.where(first_core, theirs, mine)], axis=0
    ).astype(jnp.bfloat16)

    def row_block(at, cols):
        return rows.at[
            core,
            at.get("x", slice(None)),
            at.get("y", slice(None)),
            at.get("z", slice(None)),
            slice(None),
            span(cols),
        ]

    shared = []
    for phase in range(3):
        opened = {}
        for rotation in range(3):
            dims = ORDERS[rotation]
            dim = dims[phase]
            first, second = GATHER_COLS[rotation]
            fixed = {later: pos[later] for later in dims[phase:]}
            up, down = device(dim, above(dim)), device(dim, below(dim))
            one, two = row_block(fixed, first), row_block(fixed, second)
            opened[rotation] = (
                send(one, one, up),
                send(two, two, down),
                send(two, two, up),
                send(one, one, down),
            )
            if phase == 2:
                whole = row_block(fixed, (first[0], first[1] + second[1]))
                shared.append(send(whole, whole, partner))
        forwarded = {}
        for rotation in range(3):
            dims = ORDERS[rotation]
            dim = dims[phase]
            first, second = GATHER_COLS[rotation]
            fixed = {later: pos[later] for later in dims[phase:]}
            up, down = device(dim, above(dim)), device(dim, below(dim))
            opened[rotation][0].wait_recv()
            one = row_block({**fixed, dim: below(dim)}, first)
            opened[rotation][1].wait_recv()
            two = row_block({**fixed, dim: above(dim)}, second)
            forwarded[rotation] = (send(one, one, up), send(two, two, down))
        for rotation in range(3):
            dims = ORDERS[rotation]
            dim = dims[phase]
            first, second = GATHER_COLS[rotation]
            fixed = {later: pos[later] for later in dims[phase:]}
            opened[rotation][2].wait_recv()
            opened[rotation][3].wait_recv()
            if phase == 2:
                for place in (below(dim), above(dim)):
                    whole = row_block({**fixed, dim: place}, (first[0], first[1] + second[1]))
                    shared.append(send(whole, whole, partner))
        for rotation in range(3):
            dims = ORDERS[rotation]
            dim = dims[phase]
            first, second = GATHER_COLS[rotation]
            fixed = {later: pos[later] for later in dims[phase:]}
            forwarded[rotation][0].wait_recv()
            forwarded[rotation][1].wait_recv()
            if phase == 2:
                whole = row_block({**fixed, dim: across(dim)}, (first[0], first[1] + second[1]))
                shared.append(send(whole, whole, partner))
    for copy in shared:
        copy.wait_recv()

    loads[1].wait()
    loads[2].wait()
    gate_acc[...] = jnp.zeros_like(gate_acc)
    up_acc[...] = jnp.zeros_like(up_acc)
    depth = 512
    for half in range(2):

        def product(step, carry):
            at = pl.multiple_of(step * depth, depth)
            row = pl.multiple_of(half * HALF + step * depth, depth)
            lhs = rows[half, :, :, :, :, pl.ds(at, depth)].reshape(512, depth)
            gate_acc[...] += jnp.dot(
                lhs, w_gate[pl.ds(row, depth), :], preferred_element_type=jnp.float32
            )
            up_acc[...] += jnp.dot(
                lhs, w_up[pl.ds(row, depth), :], preferred_element_type=jnp.float32
            )
            return carry

        lax.fori_loop(0, HALF // depth, product, 0)
    expert = (pos["z"] * 2 + x_lo) * 4 + pos["y"]
    parts = rows[0, :, :, :, :, HALF : HALF + 128].astype(jnp.float32).reshape(512, 128)
    lane = lax.broadcasted_iota(jnp.int32, parts.shape, 1)
    picked = jnp.where((lane == expert) | (lane == expert + 32), parts, 0.0)
    row_gate = jnp.sum(picked, axis=1, keepdims=True)
    gate_part = gate_acc[...]
    active[...] = (gate_part * jax.nn.sigmoid(gate_part) * up_acc[...] * row_gate).astype(
        jnp.bfloat16
    )

    loads[3].wait()

    def mix_units(cols, half, store):
        for start in range(cols[0], cols[0] + cols[1], UNIT):
            at = pl.multiple_of(half * HALF + start, 128)
            part = jnp.dot(
                active[...], w_down[:, pl.ds(at, UNIT)], preferred_element_type=jnp.float32
            ).reshape(4, 4, 4, 8, UNIT)
            store(start, part)

    for rotation in range(3):
        for part in range(2):
            cols = MIX_COLS[rotation][part]

            def store_out(start, value):
                mix_out[:, :, :, :, pl.ds(start, UNIT)] = value.astype(jnp.bfloat16)

            mix_units(cols, other, store_out)
            piece = (slice(None), slice(None), slice(None), slice(None), span(cols))
            handed[rotation, part] = send(mix_out.at[piece], mix_in.at[piece], partner)

    def mix_block(rotation, phase):
        dims = ORDERS[rotation][::-1]

        def block(place, cols):
            at = {}
            for earlier in dims[:phase]:
                at[earlier] = pos[earlier]
            at[dims[phase]] = place
            return mix_sum.at[
                at.get("x", slice(None)),
                at.get("y", slice(None)),
                at.get("z", slice(None)),
                slice(None),
                span(cols),
            ]

        return block

    def mix_land(rotation, phase):
        land = (mix_land0, mix_land1, mix_land2)[phase]

        def place(slot, cols):
            return land.at[
                (rotation, slot) + (slice(None),) * (3 - phase) + (pl.ds(0, cols[1]),)
            ]

        return place

    started = {}
    for rotation in range(3):
        for part in range(2):
            cols = MIX_COLS[rotation][part]
            handed[rotation, part].wait_recv()

            def store_sum(start, value):
                at = (slice(None), slice(None), slice(None), slice(None), pl.ds(start, UNIT))
                total = value + mix_in[at].astype(jnp.float32)
                mix_sum[at] = total.astype(jnp.bfloat16)

            mix_units(cols, core, store_sum)
            started[rotation, part] = ring_start(
                ORDERS[rotation][2], mix_block(rotation, 0), mix_land(rotation, 0), MIX_COLS[rotation], part
            )
    for phase in range(3):
        relayed = {}
        for rotation in range(3):
            relayed[rotation] = ring_relay(
                ORDERS[rotation][2 - phase],
                mix_block(rotation, phase),
                mix_land(rotation, phase),
                MIX_COLS[rotation],
                (started[rotation, 0], started[rotation, 1]),
            )
        for rotation in range(3):
            dim = ORDERS[rotation][2 - phase]
            block = mix_block(rotation, phase)

            def store(cols, total):
                if phase == 2:
                    attn_own[:, span(cols)] = total
                else:
                    block(pos[dim], cols)[...] = total.astype(jnp.bfloat16)

            ring_finish(
                dim,
                block,
                mix_land(rotation, phase),
                MIX_COLS[rotation],
                (started[rotation, 0], started[rotation, 1]),
                relayed[rotation],
                store,
            )
            if phase < 2:
                for part in range(2):
                    started[rotation, part] = ring_start(
                        ORDERS[rotation][1 - phase],
                        mix_block(rotation, phase + 1),
                        mix_land(rotation, phase + 1),
                        MIX_COLS[rotation],
                        part,
                    )
    swapped.wait_send()
    low, high, _ = swap_halves(attn_own)
    out_ref[:, 0:HALF] += low
    out_ref[:, HALF : 2 * HALF] += high
    for copy in sent:
        if copy is not swapped:
            copy.wait_send()


def layer_tail(values, residual, norm_gain, row_gates, out_proj, w_gate, w_up, w_down):
    bf16, f32 = jnp.bfloat16, jnp.float32
    vmem = pl.BlockSpec(memory_space=pltpu.VMEM)
    hbm = pl.BlockSpec(memory_space=pl.ANY)
    return pl.pallas_call(
        tail_kernel,
        out_shape=jax.ShapeDtypeStruct((4, 2 * HALF), f32),
        in_specs=[vmem] * 4 + [hbm] * 4,
        out_specs=vmem,
        scratch_shapes=[
            pltpu.VMEM(out_proj.shape, bf16),
            pltpu.VMEM(w_gate.shape, bf16),
            pltpu.VMEM(w_up.shape, bf16),
            pltpu.VMEM(w_down.shape, bf16),
            pltpu.VMEM((4, 2, 4, 8, HALF), bf16),
            pltpu.VMEM((4, 2, 4, 8, HALF), bf16),
            pltpu.VMEM((4, 2, 4, 8, HALF), bf16),
            pltpu.VMEM((6, 2, 4, 8, 1024), bf16),
            pltpu.VMEM((6, 4, 2, 8, 1024), bf16),
            pltpu.VMEM((2, 6, 2, 8, 1024), bf16),
            pltpu.VMEM((8, HALF), bf16),
            pltpu.VMEM((8, HALF), f32),
            pltpu.VMEM((4, HALF), f32),
            pltpu.VMEM((2, 4, HALF), f32),
            pltpu.VMEM((2, 4, HALF + 128), bf16),
            pltpu.VMEM((4, HALF + 128), bf16),
            pltpu.VMEM((2, 4, 4, 4, 8, HALF + 128), bf16),
            pltpu.VMEM((512, 256), f32),
            pltpu.VMEM((512, 256), f32),
            pltpu.VMEM((512, 256), bf16),
            pltpu.VMEM((4, 4, 4, 8, HALF), bf16),
            pltpu.VMEM((4, 4, 4, 8, HALF), bf16),
            pltpu.VMEM((4, 4, 4, 8, HALF), bf16),
            pltpu.VMEM((3, 6, 4, 4, 8, 768), bf16),
            pltpu.VMEM((3, 6, 4, 8, 768), bf16),
            pltpu.VMEM((3, 6, 8, 768), bf16),
            pltpu.SemaphoreType.DMA((4,)),
            pltpu.SemaphoreType.DMA((170,)),
            pltpu.SemaphoreType.DMA((170,)),
        ],
        compiler_params=pltpu.CompilerParams(
            collective_id=0, has_side_effects=True, vmem_limit_bytes=63 * 1024 * 1024
        ),
    )(values, residual, norm_gain, row_gates, out_proj, w_gate, w_up, w_down).astype(bf16)


def local(
    query_latent,
    query_rope,
    cache_latent,
    cache_rope,
    lengths,
    value_up,
    out_proj,
    residual,
    norm_gain,
    expert_ids,
    gate_values,
    w_gate,
    w_up,
    w_down,
):
    mixed_latent = attend(query_latent, query_rope, cache_latent, cache_rope, lengths)
    by_head = lax.all_to_all(mixed_latent, DEV, split_axis=1, concat_axis=0, tiled=True)
    head_values = jnp.einsum(
        "thl,hlv->thv", by_head, value_up, preferred_element_type=jnp.float32
    ).astype(jnp.bfloat16)
    flat_values = head_values.reshape(4, 2, 4, 8, 256)
    experts = lax.axis_size(DEV) // 2
    expert_range = jnp.arange(128, dtype=jnp.int32) % experts
    chosen = expert_ids[:, :, None] == expert_range[None, None, :]
    row_gates = jnp.sum(jnp.where(chosen, gate_values[:, :, None], 0.0), axis=1)
    return layer_tail(
        flat_values,
        residual,
        norm_gain[None, :],
        row_gates,
        out_proj,
        w_gate[0],
        w_up[0],
        w_down[0],
    )


def solution(mesh):
    finer = Mesh(
        mesh.devices.reshape(mesh.shape["group"], 4, 2, 4, 2),
        ("group", "dev_0", "dev_1", "dev_2", "dev_3"),
    )
    return jax.shard_map(
        local,
        mesh=finer,
        in_specs=(
            P(GROUP_DEV, None, None),
            P(GROUP_DEV, None, None),
            P(GROUP_DEV, None, None),
            P(GROUP_DEV, None, None),
            P(GROUP_DEV),
            P(DEV, None, None),
            P(DEV, None),
            P(GROUP_DEV, None),
            P(),
            P(GROUP_DEV, None),
            P(GROUP_DEV, None),
            P(DEV, None, "group"),
            P(DEV, None, "group"),
            P(DEV, "group", None),
        ),
        out_specs=P(GROUP_DEV, None),
        check_vma=False,
    )
```

time: 1020 us -> 149 us (0.15)
  waiting for transfers between devices: 739 us -> 11.7 us
  blocking collectives: 201 us -> 0 us
  Pallas kernels: 0 us -> 102 us
  matrix products: 43.1 us -> 16.3 us
  between operations: 14 us -> 0.14 us
  local copies, waits for them, and re-layouts: 16.6 us -> 4.31 us
  starting transfers between devices: 0.09 us -> 10.9 us
    unnamed x5 -> x0, waiting for transfers between devices: 716 us -> none
    all_gather x1 -> x0, blocking collectives: 178 us -> none  [local(): all_gates = lax.all_gather(row_gates, GROUP_DEV, axis=0, tiled=True)]
    pallas_call x0 -> x1, Pallas kernels: none -> 102 us  [layer_tail(): pl.pallas_call(tail_kernel, out_shape=jax.ShapeDtypeStruct((4, 2 * HALF),...]
    dot_general x3 -> x0, matrix products: 27.3 us -> none  [the longest x1 16.1 us: expert_rows(): return jnp.dot(active, w_down[0], preferred_element_type=jnp.float32)]
    all_gather x1 -> x0, waiting for transfers between devices: 23.3 us -> none  [local(): all_rows = lax.all_gather(normed, GROUP_DEV, axis=0, tiled=True)]
    all_to_all x1 -> x0, blocking collectives: 23.2 us -> none  [local(): lax.all_to_all(mixed_latent, DEV, split_axis=1, concat_axis=0, tiled=True)]
    unnamed x24 -> x12, local copies, waits for them, and re-layouts: 15.9 us -> 1.94 us
    all_to_all x0 -> x1, waiting for transfers between devices: none -> 11.7 us  [local(): lax.all_to_all(mixed_latent, DEV, split_axis=1, concat_axis=0, tiled=True)]
  transfers between devices with their start and end apart: 3 -> 1, of which waited for: 3 -> 1; matrix products, arithmetic and copies ran while one was open for 0% -> 0% of each run, Pallas kernels for 0% -> 0%
where the time goes in v2:
time: 149 us; the launch traced here: 148 us
  Pallas kernels  102 us (68%)
  matrix products  16.3 us (11%)
  waiting for transfers between devices  11.7 us (8%)
  starting transfers between devices  10.9 us (7%)
  local copies, waits for them, and re-layouts  4.31 us (3%)
  other arithmetic  3.03 us (2%)
    pallas_call x1, Pallas kernels, layer_tail(): pl.pallas_call(tail_kernel, out_shape=jax.ShapeDtypeStruct((4, 2 * HALF),...  102 us
    all_to_all x1, waiting for transfers between devices, local(): lax.all_to_all(mixed_latent, DEV, split_axis=1, concat_axis=0, tiled=True)  11.7 us
    all_to_all x1, starting transfers between devices, local(): lax.all_to_all(mixed_latent, DEV, split_axis=1, concat_axis=0, tiled=True)  10.9 us
    dot_general x1, matrix products, attend(): jnp.einsum('thc,tcl->thl', attn_weights, cache_latent, preferred_element_...  7.63 us
    dot_general x1, matrix products, attend(): jnp.einsum('thl,tcl->thc', query_latent, cache_latent, preferred_element_...  6.28 us
  transfers between devices with their start and end apart: 1, of which 1 were waited for; matrix products, arithmetic and copies ran while one was open for 0% of the time, Pallas kernels for 0%

profile of v2, /device:TPU:1, one launch (start us, length us, event | category | flops | bytes accessed | tf_op | source)
XLA Modules:
  0.0 148.5 jit_solution(9547714263133253348)
XLA Ops:
  0.0 0.0 copy-start
  0.0 0.0 copy-start.5
  0.0 2.1 %fusion.7 = f32[4,128,2048]{2,1,0:T(8,128)S(1)} fusion(bf16[4,128,64]{1,2,0:T(8,128)(2,1)} %param.15, bf16[4,64,2048]{2,1,0:T(8,128)(2,1)} %param.17), kind=kOutput, calls=%fused_computation.15 | convolution fusion | flops 134217728 | bytes 5308416 | tf_op jit(solution)/shard_map/thr,trc->thc/dot_general | solution.py:23
  2.1 0.0 copy-done
  2.1 0.0 copy-done.5
  2.1 6.3 %multiply_select_fusion = f32[4,128,2048]{2,1,0:T(8,128)S(1)} fusion(f32[4,128,2048]{2,1,0:T(8,128)S(1)} %fusion.7, bf16[4,128,512]{2,1,0:T(8,128)(2,1)S(1)} %copy-done, bf16[4,2048,512]{2,1,0:T(8,128)(2,1)} %param.16, s32[4]{0:T(128)S(1)} %copy-done.5), kind=kOutput, calls=%fused_computation.3 | convolution fusion | flops 1077936128 | bytes 17301520 | tf_op jit(solution)/shard_map/thl,tcl->thc/dot_general | solution.py:20
  8.4 0.0 copy-start.1
  8.4 1.9 %copy-done.1 = f32[4,128,2048]{2,1,0:T(8,128)} copy-done((f32[4,128,2048]{2,1,0:T(8,128)}, f32[4,128,2048]{2,1,0:T(8,128)S(1)}, u32[]{:S(2)}) %copy-start.1) | copy-done | bytes 4194328
  10.3 0.8 fusion.6
  11.1 0.0 copy-start.3
  11.1 0.0 copy-start.4
  11.1 7.6 %fusion.3 = bf16[4,128,512]{2,1,0:T(8,128)(2,1)S(1)} fusion(bf16[4,2048,512]{2,1,0:T(8,128)(2,1)} %param.16, f32[4,128]{1,0:T(4,128)S(1)} %fusion.6, f32[4,128,2048]{2,1,0:T(8,128)} %copy-done.1), kind=kOutput, calls=%fused_computation.7 | convolution fusion | flops 1077152256 | bytes 13109248 | tf_op jit(solution)/shard_map/thc,tcl->thl/dot_general | solution.py:32
  18.8 0.0 copy-start.2
  18.8 1.2 copy.20
  20.0 10.9 %all-to-all-start = ((bf16[4,128,512]{2,0,1:T(4,128)(2,1)}), bf16[4,128,512]{2,0,1:T(4,128)(2,1)S(1)}, u32[]{:S(2)}, u32[]{:S(2)}) async-start(bf16[4,128,512]{2,0,1:T(4,128)(2,1)} %copy.20), calls=%async_computation | async-start | bytes 1048576 | tf_op jit(solution)/shard_map/all_to_all | solution.py:607
  30.9 0.0 copy-done.3
  30.9 0.0 copy-done.4
  31.0 0.7 select_reduce_fusion.gates_ref
  31.6 11.7 %all-to-all-done = bf16[4,128,512]{2,0,1:T(4,128)(2,1)S(1)} async-done(((bf16[4,128,512]{2,0,1:T(4,128)(2,1)}), bf16[4,128,512]{2,0,1:T(4,128)(2,1)S(1)}, u32[]{:S(2)}, u32[]{:S(2)}) %all-to-all-start) | async-done | bytes 524320 | tf_op jit(solution)/shard_map/all_to_all | solution.py:607
  43.4 0.2 copy.24
  43.6 0.1 all_to_all.16
  43.7 0.0 copy-done.2
  43.7 0.3 fusion.4
  44.0 0.1 copy.22
  44.1 0.7 reshape.17.values_ref
  44.9 102.1 %shard_map.136 = f32[4,7168]{1,0:T(4,128)} custom-call(bf16[4,2,4,8,256]{4,3,2,1,0:T(8,128)(2,1)} %reshape.17.values_ref, bf16[4,7168]{1,0:T(4,128)(2,1)} %residual_ref.1, f32[1,7168]{1,0:T(1,128)} %bitcast.26, f32[4,128]{1,0:T(4,128)} %select_reduce_fusion.gates_ref, bf16[256,7168]{1,0:T(8,128)(2,1)} %proj_hbm.1, bf16[7168,256]{1,0:T(8,128)(2,1)} %bitcast.21, ...), custom_call_target="tpu_custom_call" | custom-call | tf_op jit(solution)/shard_map/pallas_call | solution.py:548
  146.9 1.5 %convert_element_type.19 = bf16[4,7168]{1,0:T(4,128)(2,1)} convert(f32[4,7168]{1,0:T(4,128)} %shard_map.136) | non-fusion elementwise | flops 28672 | bytes 172032 | tf_op jit(solution)/shard_map/convert_element_type | solution.py:587
  (1 shorter events, 0.0 us)
Async XLA Ops:
  0.0 2.1 %copy-start = (bf16[4,128,512]{2,1,0:T(8,128)(2,1)S(1)}, bf16[4,128,512]{2,1,0:T(8,128)(2,1)}, u32[]{:S(2)}) copy-start(bf16[4,128,512]{2,1,0:T(8,128)(2,1)} %param.14) | copy-start | bytes 1572868
  0.0 2.1 %copy-start.5 = (s32[4]{0:T(128)S(1)}, s32[4]{0:T(128)}, u32[]{:S(2)}) copy-start(s32[4]{0:T(128)} %param.18) | copy-start | bytes 52
  8.4 1.9 %copy-start.1 = (f32[4,128,2048]{2,1,0:T(8,128)}, f32[4,128,2048]{2,1,0:T(8,128)S(1)}, u32[]{:S(2)}) copy-start(f32[4,128,2048]{2,1,0:T(8,128)S(1)} %multiply_select_fusion) | copy-start | bytes 12582916
  11.1 19.8 %copy-start.3 = (f32[4,8]{1,0:T(4,128)S(1)}, f32[4,8]{1,0:T(4,128)}, u32[]{:S(2)}) copy-start(f32[4,8]{1,0:T(4,128)} %param.24) | copy-start | bytes 388
  11.1 19.8 %copy-start.4 = (s32[4,8]{1,0:T(4,128)S(1)}, s32[4,8]{1,0:T(4,128)}, u32[]{:S(2)}) copy-start(s32[4,8]{1,0:T(4,128)} %param.23) | copy-start | bytes 388
  18.8 24.9 %copy-start.2 = (bf16[2,512,128]{2,1,0:T(8,128)(2,1)S(1)}, bf16[2,512,128]{2,1,0:T(8,128)(2,1)}, u32[]{:S(2)}) copy-start(bf16[2,512,128]{2,1,0:T(8,128)(2,1)} %param.19) | copy-start | bytes 786436
  20.0 23.4 %all-to-all-start = ((bf16[4,128,512]{2,0,1:T(4,128)(2,1)}), bf16[4,128,512]{2,0,1:T(4,128)(2,1)S(1)}, u32[]{:S(2)}, u32[]{:S(2)}) async-start(bf16[4,128,512]{2,0,1:T(4,128)(2,1)} %copy.20), calls=%async_computation | async-start | bytes 1048576 | tf_op jit(solution)/shard_map/all_to_all | solution.py:607

commit v3 on v2

--- a/solution.py
+++ b/solution.py
@@ -16,24 +16,6 @@
 softmax_scale = 192.0 ** (-0.5)
 
 
-def attend(query_latent, query_rope, cache_latent, cache_rope, lengths):
-    scores = jnp.einsum(
-        "thl,tcl->thc", query_latent, cache_latent, preferred_element_type=jnp.float32
-    )
-    scores = scores + jnp.einsum(
-        "thr,trc->thc", query_rope, cache_rope, preferred_element_type=jnp.float32
-    )
-    scores = scores * softmax_scale
-    positions = lax.broadcasted_iota(jnp.int32, scores.shape, 2)
-    scores = jnp.where(positions < lengths[:, None, None], scores, -jnp.inf)
-    row_peak = jnp.max(scores, axis=2, keepdims=True)
-    weights = jnp.exp(scores - row_peak)
-    attn_weights = (weights / jnp.sum(weights, axis=2, keepdims=True)).astype(jnp.bfloat16)
-    return jnp.einsum(
-        "thc,tcl->thl", attn_weights, cache_latent, preferred_element_type=jnp.float32
-    ).astype(jnp.bfloat16)
-
-
 HALF = 3584
 UNIT = 256
 ATTN_COLS = (((0, 1024), (1024, 768)), ((1792, 1024), (2816, 768)))
@@ -43,16 +25,34 @@
 ORDERS = (("z", "y", "x"), ("y", "x", "z"), ("x", "z", "y"))
 
 
-def tail_kernel(
-    values_ref,
+def layer_kernel(
+    lengths_ref,
     residual_ref,
     gain_ref,
     gates_ref,
+    query_hbm,
+    query_rope_hbm,
+    cache_hbm,
+    cache_rope_hbm,
+    value_hbm,
     proj_hbm,
     gate_hbm,
     up_hbm,
     down_hbm,
     out_ref,
+    query,
+    query_rope,
+    cache,
+    cache_rope,
+    scores,
+    probs,
+    latent_out,
+    latent_in,
+    value_up,
+    even_part,
+    odd_part,
+    even_values,
+    odd_values,
     proj,
     w_gate,
     w_up,
@@ -79,7 +79,10 @@
     mix_land0,
     mix_land1,
     mix_land2,
+    cache_sem,
     load_sem,
+    latent_send,
+    latent_recv,
     send_sem,
     recv_sem,
 ):
@@ -124,20 +127,125 @@
         sent.append(copy)
         return copy
 
-    loads = []
-    for number, (src, dst) in enumerate(
-        ((proj_hbm, proj), (gate_hbm, w_gate), (up_hbm, w_up), (down_hbm, w_down))
-    ):
-        load = pltpu.make_async_copy(src, dst, load_sem.at[number])
-        load.start()
-        loads.append(load)
+    def load(number, src, dst):
+        copy = pltpu.make_async_copy(src, dst, load_sem.at[number])
+        copy.start()
+        return copy
+
+    def load_cache(token):
+        slot = token % 2
+        copy = pltpu.make_async_copy(cache_hbm.at[token], cache.at[slot], cache_sem.at[slot])
+        copy.start()
+        return copy
+
+    query_load = load(4, query_hbm, query)
+    query_rope_load = load(5, query_rope_hbm, query_rope)
+    cache_loads = [load_cache(0)]
+    cache_rope_load = load(6, cache_rope_hbm, cache_rope)
+    cache_loads.append(load_cache(1))
+
+    place = ((pos["z"] * 2 + x_lo) * 4 + pos["y"]) * 2 + core
+
+    def peer(step):
+        number = lax.rem(place + step, 64)
+        return number, {
+            "dev_0": lax.div(number, 16),
+            "dev_1": lax.rem(lax.div(number, 8), 2),
+            "dev_2": lax.rem(lax.div(number, 2), 4),
+            "dev_3": lax.rem(number, 2),
+        }
 
     barrier = pltpu.get_barrier_semaphore()
-    pl.semaphore_signal(barrier, inc=1, device_id=partner, device_id_type=MESH)
-    for dim in ("x", "y", "z"):
-        for place in (above(dim), below(dim)):
-            pl.semaphore_signal(barrier, inc=1, device_id=device(dim, place), device_id_type=MESH)
-    pl.semaphore_wait(barrier, 7)
+
+    def greet(step, carry):
+        pl.semaphore_signal(barrier, inc=1, device_id=peer(step)[1], device_id_type=MESH)
+        return carry
+
+    lax.fori_loop(1, 64, greet, 0)
+    outer_x = lax.rem(pos["x"] + 3 + 2 * x_lo, 4)
+    pl.semaphore_signal(barrier, inc=1, device_id=device("x", outer_x), device_id_type=MESH)
+
+    query_load.wait()
+    query_rope_load.wait()
+    loads = {}
+    for token in range(4):
+        slot = token % 2
+        cache_loads[token].wait()
+        if token == 0:
+            cache_rope_load.wait()
+            loads["value"] = load(7, value_hbm, value_up)
+            loads["proj"] = load(0, proj_hbm, proj)
+        length = lengths_ref[token]
+        peak = jnp.full((128, 1), -jnp.inf, jnp.float32)
+        for start in range(0, 2048, 512):
+            cols = pl.ds(start, 512)
+            part = lax.dot_general(
+                query[token],
+                cache[slot, cols, :],
+                (((1,), (1,)), ((), ())),
+                preferred_element_type=jnp.float32,
+            ) + lax.dot_general(
+                query_rope[token],
+                cache_rope[token, :, cols],
+                (((0,), (0,)), ((), ())),
+                preferred_element_type=jnp.float32,
+            )
+            slots = lax.broadcasted_iota(jnp.int32, part.shape, 1) + start
+            part = jnp.where(slots < length, part, -jnp.inf)
+            scores[:, cols] = part
+            peak = jnp.maximum(peak, jnp.max(part, axis=1, keepdims=True))
+        total = jnp.zeros((128, 1), jnp.float32)
+        for start in range(0, 2048, 512):
+            cols = pl.ds(start, 512)
+            weights = jnp.exp((scores[:, cols] - peak) * softmax_scale)
+            total = total + jnp.sum(weights, axis=1, keepdims=True)
+            probs[:, cols] = weights.astype(jnp.bfloat16)
+        mixed = jnp.dot(probs[...], cache[slot], preferred_element_type=jnp.float32) / total
+        latent_out[token] = mixed.reshape(64, 2, 512).astype(jnp.bfloat16)
+        if token + 2 < 4:
+            cache_loads.append(load_cache(token + 2))
+        if token == 0:
+            pl.semaphore_wait(barrier, 64)
+        elif token == 1:
+            loads["gate"] = load(1, gate_hbm, w_gate)
+        elif token == 2:
+            loads["up"] = load(2, up_hbm, w_up)
+            loads["down"] = load(3, down_hbm, w_down)
+
+        def scatter(step, carry):
+            number, to = peer(step)
+            pltpu.make_async_remote_copy(
+                src_ref=latent_out.at[token, number],
+                dst_ref=latent_in.at[token, place],
+                send_sem=latent_send.at[token],
+                recv_sem=latent_recv.at[token],
+                device_id=to,
+                device_id_type=MESH,
+            ).start()
+            return carry
+
+        lax.fori_loop(1, 64, scatter, 0)
+        latent_in[token, place] = latent_out[token, place]
+
+    def latent_copies(token):
+        return pltpu.make_async_remote_copy(
+            src_ref=latent_out.at[token, pl.ds(0, 63)],
+            dst_ref=latent_in.at[token, pl.ds(0, 63)],
+            send_sem=latent_send.at[token],
+            recv_sem=latent_recv.at[token],
+            device_id=partner,
+            device_id_type=MESH,
+        )
+
+    loads["value"].wait()
+    for token in range(4):
+        latent_copies(token).wait_recv()
+        latents = latent_in[token].reshape(128, 512)
+        even_part[...] = jnp.dot(latents, value_up[0], preferred_element_type=jnp.float32)
+        odd_part[...] = jnp.dot(latents, value_up[1], preferred_element_type=jnp.float32)
+        even_values[pl.ds(token, 64, stride=4), :] = even_part[pl.ds(0, 64, stride=2), :]
+        odd_values[pl.ds(token, 64, stride=4), :] = odd_part[pl.ds(1, 64, stride=2), :]
+    values = jnp.concatenate([even_values[...], odd_values[...]], axis=1).astype(jnp.bfloat16)
 
     def ring_start(dim, block, land, cols, part):
         first, second = cols
@@ -195,8 +303,7 @@
 
     swap_count = [0]
 
-    values = values_ref[...].reshape(256, 256)
-    loads[0].wait()
+    loads["proj"].wait()
     handed = {}
 
     def attn_units(cols, half, store):
@@ -400,8 +507,8 @@
     for copy in shared:
         copy.wait_recv()
 
-    loads[1].wait()
-    loads[2].wait()
+    loads["gate"].wait()
+    loads["up"].wait()
     gate_acc[...] = jnp.zeros_like(gate_acc)
     up_acc[...] = jnp.zeros_like(up_acc)
     depth = 512
@@ -430,7 +537,7 @@
         jnp.bfloat16
     )
 
-    loads[3].wait()
+    loads["down"].wait()
 
     def mix_units(cols, half, store):
         for start in range(cols[0], cols[0] + cols[1], UNIT):
@@ -539,18 +646,47 @@
     for copy in sent:
         if copy is not swapped:
             copy.wait_send()
-
-
-def layer_tail(values, residual, norm_gain, row_gates, out_proj, w_gate, w_up, w_down):
+    for token in range(4):
+        latent_copies(token).wait_send()
+
+
+def layer(
+    lengths,
+    residual,
+    norm_gain,
+    row_gates,
+    query_latent,
+    query_rope,
+    cache_latent,
+    cache_rope,
+    value_up,
+    out_proj,
+    w_gate,
+    w_up,
+    w_down,
+):
     bf16, f32 = jnp.bfloat16, jnp.float32
     vmem = pl.BlockSpec(memory_space=pltpu.VMEM)
     hbm = pl.BlockSpec(memory_space=pl.ANY)
     return pl.pallas_call(
-        tail_kernel,
+        layer_kernel,
         out_shape=jax.ShapeDtypeStruct((4, 2 * HALF), f32),
-        in_specs=[vmem] * 4 + [hbm] * 4,
+        in_specs=[pl.BlockSpec(memory_space=pltpu.SMEM)] + [vmem] * 3 + [hbm] * 9,
         out_specs=vmem,
         scratch_shapes=[
+            pltpu.VMEM(query_latent.shape, bf16),
+            pltpu.VMEM(query_rope.shape, bf16),
+            pltpu.VMEM((2, 2048, 512), bf16),
+            pltpu.VMEM(cache_rope.shape, bf16),
+            pltpu.VMEM((128, 2048), f32),
+            pltpu.VMEM((128, 2048), bf16),
+            pltpu.VMEM((4, 64, 2, 512), bf16),
+            pltpu.VMEM((4, 64, 2, 512), bf16),
+            pltpu.VMEM(value_up.shape, bf16),
+            pltpu.VMEM((128, 128), f32),
+            pltpu.VMEM((128, 128), f32),
+            pltpu.VMEM((256, 128), f32),
+            pltpu.VMEM((256, 128), f32),
             pltpu.VMEM(out_proj.shape, bf16),
             pltpu.VMEM(w_gate.shape, bf16),
             pltpu.VMEM(w_up.shape, bf16),
@@ -577,6 +713,9 @@
             pltpu.VMEM((3, 6, 4, 4, 8, 768), bf16),
             pltpu.VMEM((3, 6, 4, 8, 768), bf16),
             pltpu.VMEM((3, 6, 8, 768), bf16),
+            pltpu.SemaphoreType.DMA((2,)),
+            pltpu.SemaphoreType.DMA((8,)),
+            pltpu.SemaphoreType.DMA((4,)),
             pltpu.SemaphoreType.DMA((4,)),
             pltpu.SemaphoreType.DMA((170,)),
             pltpu.SemaphoreType.DMA((170,)),
@@ -584,7 +723,21 @@
         compiler_params=pltpu.CompilerParams(
             collective_id=0, has_side_effects=True, vmem_limit_bytes=63 * 1024 * 1024
         ),
-    )(values, residual, norm_gain, row_gates, out_proj, w_gate, w_up, w_down).astype(bf16)
+    )(
+        lengths,
+        residual,
+        norm_gain,
+        row_gates,
+        query_latent,
+        query_rope,
+        cache_latent,
+        cache_rope,
+        value_up,
+        out_proj,
+        w_gate,
+        w_up,
+        w_down,
+    ).astype(bf16)
 
 
 def local(
@@ -603,21 +756,20 @@
     w_up,
     w_down,
 ):
-    mixed_latent = attend(query_latent, query_rope, cache_latent, cache_rope, lengths)
-    by_head = lax.all_to_all(mixed_latent, DEV, split_axis=1, concat_axis=0, tiled=True)
-    head_values = jnp.einsum(
-        "thl,hlv->thv", by_head, value_up, preferred_element_type=jnp.float32
-    ).astype(jnp.bfloat16)
-    flat_values = head_values.reshape(4, 2, 4, 8, 256)
     experts = lax.axis_size(DEV) // 2
     expert_range = jnp.arange(128, dtype=jnp.int32) % experts
     chosen = expert_ids[:, :, None] == expert_range[None, None, :]
     row_gates = jnp.sum(jnp.where(chosen, gate_values[:, :, None], 0.0), axis=1)
-    return layer_tail(
-        flat_values,
+    return layer(
+        lengths,
         residual,
         norm_gain[None, :],
         row_gates,
+        query_latent,
+        jnp.swapaxes(query_rope, 1, 2),
+        cache_latent,
+        cache_rope,
+        value_up,
         out_proj,
         w_gate[0],
         w_up[0],

time: 149 us -> 129 us (0.87)
  Pallas kernels: 102 us -> 126 us
  matrix products: 16.3 us -> 0 us
  waiting for transfers between devices: 11.7 us -> 0 us
  starting transfers between devices: 10.9 us -> 0 us
  local copies, waits for them, and re-layouts: 4.31 us -> 0 us
    pallas_call x1, Pallas kernels: 102 us -> 126 us  [layer(): pl.pallas_call(layer_kernel, out_shape=jax.ShapeDtypeStruct((4, 2 * HALF)...]
    dot_general x4 -> x0, matrix products: 16.3 us -> none  [the longest x1 7.63 us: attend(): jnp.einsum('thc,tcl->thl', attn_weights, cache_latent, preferred_element_...]
    all_to_all x1 -> x0, waiting for transfers between devices: 11.7 us -> none  [local(): lax.all_to_all(mixed_latent, DEV, split_axis=1, concat_axis=0, tiled=True)]
    all_to_all x1 -> x0, starting transfers between devices: 10.9 us -> none  [local(): lax.all_to_all(mixed_latent, DEV, split_axis=1, concat_axis=0, tiled=True)]
    unnamed x12 -> x0, local copies, waits for them, and re-layouts: 1.94 us -> none
  transfers between devices with their start and end apart: 1 -> 0, of which waited for: 1 -> 0; matrix products, arithmetic and copies ran while one was open for 0% -> 0% of each run, Pallas kernels for 0% -> 0%
where the time goes in v3:
time: 129 us
  Pallas kernels  126 us (98%)
  other arithmetic  2.91 us (2%)
    pallas_call x1, Pallas kernels, layer(): pl.pallas_call(layer_kernel, out_shape=jax.ShapeDtypeStruct((4, 2 * HALF)...  126 us

profile of v3, /device:TPU:1, one launch (start us, length us, event | category | flops | bytes accessed | tf_op | source)
XLA Modules:
  0.0 128.9 jit_solution(654687580009372705)
XLA Ops:
  0.0 1.4 %select_reduce_fusion.gates_ref = f32[4,128]{1,0:T(4,128)} fusion(f32[4,8]{1,0:T(4,128)} %param.24, s32[128]{0:T(128)S(1)} %and_select_fusion, s32[4,8]{1,0:T(4,128)} %param.23), kind=kLoop, calls=%fused_computation | loop fusion | flops 11776 | bytes 2816 | tf_op jit(solution)/shard_map/reduce_sum | solution.py:762
  1.4 126.0 %shard_map.136 = f32[4,7168]{1,0:T(4,128)} custom-call(s32[4]{0:T(128)} %lengths_ref.1, bf16[4,7168]{1,0:T(4,128)(2,1)} %residual_ref.1, f32[1,7168]{1,0:T(1,128)} %bitcast.9, f32[4,128]{1,0:T(4,128)} %select_reduce_fusion.gates_ref, bf16[4,128,512]{2,1,0:T(8,128)(2,1)} %query_hbm.1, bf16[4,64,128]{2,1,0:T(8,128)(2,1)} %bitcast.8, ...), custom_call_target="tpu_custom_call" | custom-call | tf_op jit(solution)/shard_map/pallas_call | solution.py:671
  127.4 1.5 %convert_element_type.3 = bf16[4,7168]{1,0:T(4,128)(2,1)} convert(f32[4,7168]{1,0:T(4,128)} %shard_map.136) | non-fusion elementwise | flops 28672 | bytes 172032 | tf_op jit(solution)/shard_map/convert_element_type | solution.py:740
  (1 shorter events, 0.0 us)

commit v4 on v3

--- a/solution.py
+++ b/solution.py
@@ -29,7 +29,8 @@
     lengths_ref,
     residual_ref,
     gain_ref,
-    gates_ref,
+    ids_ref,
+    gate_values_ref,
     query_hbm,
     query_rope_hbm,
     cache_hbm,
@@ -46,35 +47,35 @@
     cache_rope,
     scores,
     probs,
+    latent_all,
     latent_out,
     latent_in,
     value_up,
     even_part,
     odd_part,
-    even_values,
-    odd_values,
     proj,
     w_gate,
     w_up,
     w_down,
-    attn_out,
-    attn_in,
+    values,
     attn_sum,
     attn_land0a,
     attn_land0b,
     attn_land1,
     attn_land2,
-    attn_own,
+    residual_out,
+    residual_in,
+    gates_out,
+    gates_in,
+    square_out,
+    square_in,
+    stream,
     swap_out,
     swap_in,
-    row_out,
-    row_in,
     rows,
     gate_acc,
     up_acc,
     active,
-    mix_out,
-    mix_in,
     mix_sum,
     mix_land0,
     mix_land1,
@@ -162,8 +163,24 @@
         return carry
 
     lax.fori_loop(1, 64, greet, 0)
-    outer_x = lax.rem(pos["x"] + 3 + 2 * x_lo, 4)
-    pl.semaphore_signal(barrier, inc=1, device_id=device("x", outer_x), device_id_type=MESH)
+    for far_x in (lax.rem(pos["x"] + 3 + 2 * x_lo, 4), across("x")):
+        pl.semaphore_signal(barrier, inc=1, device_id=device("x", far_x), device_id_type=MESH)
+
+    own_half = pl.ds(pl.multiple_of(core * HALF, 128), HALF)
+    other_half = pl.ds(pl.multiple_of(other * HALF, 128), HALF)
+    own_rows = pl.ds(pl.multiple_of(core * 256, 256), 256)
+    residual_out[...] = residual_ref[:, other_half]
+    lane = lax.broadcasted_iota(jnp.int32, (4, 128), 1)
+    gates = jnp.zeros((4, 128), jnp.float32)
+    for choice in range(8):
+        named = lax.rem(lane, 32) == ids_ref[:, choice : choice + 1]
+        gates = gates + jnp.where(named, gate_values_ref[:, choice : choice + 1], 0.0)
+    gates_out[...] = gates
+
+    def eight_rows(mine, theirs):
+        return jnp.concatenate(
+            [jnp.where(first_core, mine, theirs), jnp.where(first_core, theirs, mine)], axis=0
+        )
 
     query_load.wait()
     query_rope_load.wait()
@@ -174,7 +191,7 @@
         if token == 0:
             cache_rope_load.wait()
             loads["value"] = load(7, value_hbm, value_up)
-            loads["proj"] = load(0, proj_hbm, proj)
+            loads["proj"] = load(0, proj_hbm.at[:, own_half], proj.at[own_rows])
         length = lengths_ref[token]
         peak = jnp.full((128, 1), -jnp.inf, jnp.float32)
         for start in range(0, 2048, 512):
@@ -201,51 +218,56 @@
             total = total + jnp.sum(weights, axis=1, keepdims=True)
             probs[:, cols] = weights.astype(jnp.bfloat16)
         mixed = jnp.dot(probs[...], cache[slot], preferred_element_type=jnp.float32) / total
-        latent_out[token] = mixed.reshape(64, 2, 512).astype(jnp.bfloat16)
+        latent_all[:, 2 * token : 2 * token + 2, :] = mixed.reshape(64, 2, 512)
         if token + 2 < 4:
             cache_loads.append(load_cache(token + 2))
         if token == 0:
-            pl.semaphore_wait(barrier, 64)
+            pl.semaphore_wait(barrier, 65)
+            handed = {
+                "residual": send(residual_out, residual_in, partner),
+                "gates": send(gates_out, gates_in, partner),
+                "proj": send(proj_hbm.at[:, other_half], proj.at[own_rows], partner),
+            }
         elif token == 1:
             loads["gate"] = load(1, gate_hbm, w_gate)
         elif token == 2:
             loads["up"] = load(2, up_hbm, w_up)
-            loads["down"] = load(3, down_hbm, w_down)
-
-        def scatter(step, carry):
-            number, to = peer(step)
-            pltpu.make_async_remote_copy(
-                src_ref=latent_out.at[token, number],
-                dst_ref=latent_in.at[token, place],
-                send_sem=latent_send.at[token],
-                recv_sem=latent_recv.at[token],
-                device_id=to,
-                device_id_type=MESH,
-            ).start()
-            return carry
-
-        lax.fori_loop(1, 64, scatter, 0)
-        latent_in[token, place] = latent_out[token, place]
-
-    def latent_copies(token):
-        return pltpu.make_async_remote_copy(
-            src_ref=latent_out.at[token, pl.ds(0, 63)],
-            dst_ref=latent_in.at[token, pl.ds(0, 63)],
-            send_sem=latent_send.at[token],
-            recv_sem=latent_recv.at[token],
-            device_id=partner,
+            loads["down"] = load(3, down_hbm.at[:, own_half], w_down.at[own_rows])
+            handed["down"] = send(down_hbm.at[:, other_half], w_down.at[own_rows], partner)
+
+    latent_out[...] = latent_all[...].astype(jnp.bfloat16)
+
+    def scatter(step, carry):
+        number, to = peer(lax.rem(step * 19, 64))
+        pltpu.make_async_remote_copy(
+            src_ref=latent_out.at[number],
+            dst_ref=latent_in.at[place],
+            send_sem=latent_send.at[0],
+            recv_sem=latent_recv.at[0],
+            device_id=to,
             device_id_type=MESH,
-        )
+        ).start()
+        return carry
+
+    lax.fori_loop(1, 64, scatter, 0)
+    latent_in[place] = latent_out[place]
+    latent_copies = pltpu.make_async_remote_copy(
+        src_ref=latent_out.at[pl.ds(0, 63)],
+        dst_ref=latent_in.at[pl.ds(0, 63)],
+        send_sem=latent_send.at[0],
+        recv_sem=latent_recv.at[0],
+        device_id=partner,
+        device_id_type=MESH,
+    )
 
     loads["value"].wait()
-    for token in range(4):
-        latent_copies(token).wait_recv()
-        latents = latent_in[token].reshape(128, 512)
-        even_part[...] = jnp.dot(latents, value_up[0], preferred_element_type=jnp.float32)
-        odd_part[...] = jnp.dot(latents, value_up[1], preferred_element_type=jnp.float32)
-        even_values[pl.ds(token, 64, stride=4), :] = even_part[pl.ds(0, 64, stride=2), :]
-        odd_values[pl.ds(token, 64, stride=4), :] = odd_part[pl.ds(1, 64, stride=2), :]
-    values = jnp.concatenate([even_values[...], odd_values[...]], axis=1).astype(jnp.bfloat16)
+    latent_copies.wait_recv()
+    latents = latent_in[...].reshape(512, 512)
+    even_part[...] = jnp.dot(latents, value_up[0], preferred_element_type=jnp.float32)
+    odd_part[...] = jnp.dot(latents, value_up[1], preferred_element_type=jnp.float32)
+    values[core] = jnp.concatenate(
+        [even_part[pl.ds(0, 256, stride=2), :], odd_part[pl.ds(1, 256, stride=2), :]], axis=1
+    ).astype(jnp.bfloat16)
 
     def ring_start(dim, block, land, cols, part):
         first, second = cols
@@ -288,42 +310,24 @@
         relayed[1].wait_recv()
         store(second, add_into(block(pos[dim], second), land(3, second), land(5, second)))
 
+    def direct_start(dim, block, land, cols):
+        return [
+            send(block(where(dim), cols), land(slot, cols), device(dim, where(dim)))
+            for slot, where in enumerate((above, below, across))
+        ]
+
+    def direct_finish(dim, block, land, cols, started, store):
+        for copy in started:
+            copy.wait_recv()
+        store(cols, add_into(block(pos[dim], cols), *(land(slot, cols) for slot in range(3))))
+
+    def whole_cols(cols):
+        return cols[0][0], cols[0][1] + cols[1][1]
+
     def span(cols):
         return pl.ds(cols[0], cols[1])
 
-    def swap_halves(own):
-        top, bottom = own[0:4, :], own[4:8, :]
-        swap_out[...] = jnp.where(first_core, bottom, top)
-        swapped = send(swap_out, swap_in.at[swap_count[0]], partner)
-        swap_count[0] += 1
-        swapped.wait_recv()
-        mine = jnp.where(first_core, top, bottom)
-        theirs = swap_in[swap_count[0] - 1]
-        return jnp.where(first_core, mine, theirs), jnp.where(first_core, theirs, mine), swapped
-
-    swap_count = [0]
-
-    loads["proj"].wait()
-    handed = {}
-
-    def attn_units(cols, half, store):
-        for start in range(cols[0], cols[0] + cols[1], UNIT):
-            at = pl.multiple_of(half * HALF + start, 128)
-            part = jnp.dot(
-                values, proj[:, pl.ds(at, UNIT)], preferred_element_type=jnp.float32
-            ).reshape(4, 2, 4, 8, UNIT)
-            store(start, part)
-
-    for rotation in range(2):
-        for part in range(2):
-            cols = ATTN_COLS[rotation][part]
-
-            def store_out(start, value):
-                attn_out[:, :, :, :, pl.ds(start, UNIT)] = value.astype(jnp.bfloat16)
-
-            attn_units(cols, other, store_out)
-            piece = (slice(None), slice(None), slice(None), slice(None), span(cols))
-            handed[rotation, part] = send(attn_out.at[piece], attn_in.at[piece], partner)
+    handed["values"] = send(values.at[core], values.at[core], partner)
 
     def attn_block(rotation, phase):
         dims = ATTN_ORDERS[rotation]
@@ -350,96 +354,95 @@
         ]
 
     started = {}
+    loads["proj"].wait()
+    handed["proj"].wait_recv()
+    handed["values"].wait_recv()
     for rotation in range(2):
-        dim = ATTN_ORDERS[rotation][0]
         for part in range(2):
             cols = ATTN_COLS[rotation][part]
-            handed[rotation, part].wait_recv()
-
-            def store_sum(start, value):
-                at = (slice(None), slice(None), slice(None), slice(None), pl.ds(start, UNIT))
-                total = value + attn_in[at].astype(jnp.float32)
-                attn_sum[at] = total.astype(jnp.bfloat16)
-
-            attn_units(cols, core, store_sum)
+            for start in range(cols[0], cols[0] + cols[1], UNIT):
+                piece = pl.ds(start, UNIT)
+                share = jnp.dot(
+                    values[0], proj[0:256, piece], preferred_element_type=jnp.float32
+                ) + jnp.dot(values[1], proj[256:512, piece], preferred_element_type=jnp.float32)
+                attn_sum[:, :, :, :, piece] = share.reshape(4, 2, 4, 8, UNIT).astype(jnp.bfloat16)
             started[rotation, part] = ring_start(
-                dim, attn_block(rotation, 0), attn_land(rotation, 0), ATTN_COLS[rotation], part
+                ATTN_ORDERS[rotation][0],
+                attn_block(rotation, 0),
+                attn_land(rotation, 0),
+                ATTN_COLS[rotation],
+                part,
             )
+    relayed = {}
+    for rotation in range(2):
+        relayed[rotation] = ring_relay(
+            ATTN_ORDERS[rotation][0],
+            attn_block(rotation, 0),
+            attn_land(rotation, 0),
+            ATTN_COLS[rotation],
+            (started[rotation, 0], started[rotation, 1]),
+        )
+
+    def keep_in(block, dim):
+        def store(cols, total):
+            block(pos[dim], cols)[...] = total.astype(jnp.bfloat16)
+
+        return store
+
+    for rotation in range(2):
+        dim, next_dim = ATTN_ORDERS[rotation]
+        block = attn_block(rotation, 0)
+        ring_finish(
+            dim,
+            block,
+            attn_land(rotation, 0),
+            ATTN_COLS[rotation],
+            (started[rotation, 0], started[rotation, 1]),
+            relayed[rotation],
+            keep_in(block, dim),
+        )
+        started[rotation] = direct_start(
+            next_dim, attn_block(rotation, 1), attn_land(rotation, 1), whole_cols(ATTN_COLS[rotation])
+        )
     paired = {}
-    for phase in range(2):
-        relayed = {}
-        for rotation in range(2):
-            relayed[rotation] = ring_relay(
-                ATTN_ORDERS[rotation][phase],
-                attn_block(rotation, phase),
-                attn_land(rotation, phase),
-                ATTN_COLS[rotation],
-                (started[rotation, 0], started[rotation, 1]),
-            )
-        for rotation in range(2):
-            dim = ATTN_ORDERS[rotation][phase]
-            block = attn_block(rotation, phase)
-
-            def store(cols, total):
-                block(pos[dim], cols)[...] = total.astype(jnp.bfloat16)
-
-            ring_finish(
-                dim,
-                block,
-                attn_land(rotation, phase),
-                ATTN_COLS[rotation],
-                (started[rotation, 0], started[rotation, 1]),
-                relayed[rotation],
-                store,
-            )
-            if phase == 0:
-                for part in range(2):
-                    started[rotation, part] = ring_start(
-                        ATTN_ORDERS[rotation][1],
-                        attn_block(rotation, 1),
-                        attn_land(rotation, 1),
-                        ATTN_COLS[rotation],
-                        part,
-                    )
-            else:
-                width = ATTN_COLS[rotation][0][1] + ATTN_COLS[rotation][1][1]
-                piece = pl.ds(ATTN_COLS[rotation][0][0], width)
-                paired[rotation] = send(
-                    attn_sum.at[pos["z"], 1 - x_lo, pos["y"], slice(None), piece],
-                    attn_land2.at[slice(None), piece],
-                    x_pair,
-                )
+    for rotation in range(2):
+        dim = ATTN_ORDERS[rotation][1]
+        block = attn_block(rotation, 1)
+        cols = whole_cols(ATTN_COLS[rotation])
+        direct_finish(
+            dim, block, attn_land(rotation, 1), cols, started[rotation], keep_in(block, dim)
+        )
+        paired[rotation] = send(
+            attn_sum.at[pos["z"], 1 - x_lo, pos["y"], slice(None), span(cols)],
+            attn_land2.at[slice(None), span(cols)],
+            x_pair,
+        )
+    handed["residual"].wait_recv()
+    handed["gates"].wait_recv()
     for rotation in range(2):
         paired[rotation].wait_recv()
-    attn_own[...] = attn_sum[pos["z"], x_lo, pos["y"]].astype(jnp.float32) + attn_land2[
-        ...
-    ].astype(jnp.float32)
-    low, high, swapped = swap_halves(attn_own)
-    stream_low = residual_ref[:, 0:HALF].astype(jnp.float32) + low
-    stream_high = residual_ref[:, HALF : 2 * HALF].astype(jnp.float32) + high
-    square = jnp.sum(stream_low * stream_low, axis=1, keepdims=True) + jnp.sum(
-        stream_high * stream_high, axis=1, keepdims=True
+    residual = eight_rows(
+        residual_ref[:, own_half].astype(jnp.float32), residual_in[...].astype(jnp.float32)
     )
-    scale = lax.rsqrt(square / (2 * HALF) + 1e-06)
-    dense = gates_ref[...]
+    stream[...] = (
+        residual
+        + attn_sum[pos["z"], x_lo, pos["y"]].astype(jnp.float32)
+        + attn_land2[...].astype(jnp.float32)
+    )
+    square = jnp.sum(stream[...] * stream[...], axis=1, keepdims=True)
+    square_out[...] = jnp.broadcast_to(square, (8, 128))
+    squared = send(square_out, square_in, partner)
+    dense = eight_rows(gates_out[...], gates_in[...])
     coarse = dense.astype(jnp.bfloat16).astype(jnp.float32)
     lane = lax.broadcasted_iota(jnp.int32, dense.shape, 1)
     packed = jnp.where(lane < 32, coarse, jnp.where(lane < 64, dense - coarse, 0.0))
-    row_out[0, :, 0:HALF] = (stream_low * scale * gain_ref[:, 0:HALF]).astype(jnp.bfloat16)
-    row_out[1, :, 0:HALF] = (stream_high * scale * gain_ref[:, HALF : 2 * HALF]).astype(
-        jnp.bfloat16
-    )
-    row_out[0, :, HALF : HALF + 128] = packed.astype(jnp.bfloat16)
-    row_out[1, :, HALF : HALF + 128] = packed.astype(jnp.bfloat16)
-    handed_rows = send(row_out.at[other], row_in, partner)
-    out_ref[:, 0:HALF] = stream_low
-    out_ref[:, HALF : 2 * HALF] = stream_high
-
-    handed_rows.wait_recv()
-    mine = row_out[core].astype(jnp.float32)
-    theirs = row_in[...].astype(jnp.float32)
-    rows[core, pos["x"], pos["y"], pos["z"]] = jnp.concatenate(
-        [jnp.where(first_core, mine, theirs), jnp.where(first_core, theirs, mine)], axis=0
+    mine = (core, pos["x"], pos["y"], pos["z"])
+    rows[mine + (slice(None), pl.ds(HALF, 128))] = packed.astype(jnp.bfloat16)
+    squared.wait_recv()
+    total = square_out[:, 0:1] + square_in[:, 0:1]
+    scale = lax.rsqrt(total / (2 * HALF) + 1e-06)
+    rows[mine + (slice(None), pl.ds(0, HALF))] = (
+        stream[...] * scale * gain_ref[:, own_half]
     ).astype(jnp.bfloat16)
 
     def row_block(at, cols):
@@ -453,7 +456,17 @@
         ]
 
     shared = []
-    for phase in range(3):
+    opened = {}
+    for rotation in range(3):
+        dim = ORDERS[rotation][0]
+        own = row_block(pos, whole_cols(GATHER_COLS[rotation]))
+        opened[rotation] = [
+            send(own, own, device(dim, where(dim))) for where in (above, below, across)
+        ]
+    for rotation in range(3):
+        for copy in opened[rotation]:
+            copy.wait_recv()
+    for phase in range(1, 3):
         opened = {}
         for rotation in range(3):
             dims = ORDERS[rotation]
@@ -533,30 +546,14 @@
     picked = jnp.where((lane == expert) | (lane == expert + 32), parts, 0.0)
     row_gate = jnp.sum(picked, axis=1, keepdims=True)
     gate_part = gate_acc[...]
-    active[...] = (gate_part * jax.nn.sigmoid(gate_part) * up_acc[...] * row_gate).astype(
+    active[core] = (gate_part * jax.nn.sigmoid(gate_part) * up_acc[...] * row_gate).astype(
         jnp.bfloat16
     )
 
+    handed["active"] = send(active.at[core], active.at[core], partner)
     loads["down"].wait()
-
-    def mix_units(cols, half, store):
-        for start in range(cols[0], cols[0] + cols[1], UNIT):
-            at = pl.multiple_of(half * HALF + start, 128)
-            part = jnp.dot(
-                active[...], w_down[:, pl.ds(at, UNIT)], preferred_element_type=jnp.float32
-            ).reshape(4, 4, 4, 8, UNIT)
-            store(start, part)
-
-    for rotation in range(3):
-        for part in range(2):
-            cols = MIX_COLS[rotation][part]
-
-            def store_out(start, value):
-                mix_out[:, :, :, :, pl.ds(start, UNIT)] = value.astype(jnp.bfloat16)
-
-            mix_units(cols, other, store_out)
-            piece = (slice(None), slice(None), slice(None), slice(None), span(cols))
-            handed[rotation, part] = send(mix_out.at[piece], mix_in.at[piece], partner)
+    handed["down"].wait_recv()
+    handed["active"].wait_recv()
 
     def mix_block(rotation, phase):
         dims = ORDERS[rotation][::-1]
@@ -590,18 +587,16 @@
     for rotation in range(3):
         for part in range(2):
             cols = MIX_COLS[rotation][part]
-            handed[rotation, part].wait_recv()
-
-            def store_sum(start, value):
-                at = (slice(None), slice(None), slice(None), slice(None), pl.ds(start, UNIT))
-                total = value + mix_in[at].astype(jnp.float32)
-                mix_sum[at] = total.astype(jnp.bfloat16)
-
-            mix_units(cols, core, store_sum)
+            for start in range(cols[0], cols[0] + cols[1], UNIT):
+                piece = pl.ds(start, UNIT)
+                share = jnp.dot(
+                    active[0], w_down[0:256, piece], preferred_element_type=jnp.float32
+                ) + jnp.dot(active[1], w_down[256:512, piece], preferred_element_type=jnp.float32)
+                mix_sum[:, :, :, :, piece] = share.reshape(4, 4, 4, 8, UNIT).astype(jnp.bfloat16)
             started[rotation, part] = ring_start(
                 ORDERS[rotation][2], mix_block(rotation, 0), mix_land(rotation, 0), MIX_COLS[rotation], part
             )
-    for phase in range(3):
+    for phase in range(2):
         relayed = {}
         for rotation in range(3):
             relayed[rotation] = ring_relay(
@@ -614,13 +609,6 @@
         for rotation in range(3):
             dim = ORDERS[rotation][2 - phase]
             block = mix_block(rotation, phase)
-
-            def store(cols, total):
-                if phase == 2:
-                    attn_own[:, span(cols)] = total
-                else:
-                    block(pos[dim], cols)[...] = total.astype(jnp.bfloat16)
-
             ring_finish(
                 dim,
                 block,
@@ -628,33 +616,56 @@
                 MIX_COLS[rotation],
                 (started[rotation, 0], started[rotation, 1]),
                 relayed[rotation],
-                store,
+                keep_in(block, dim),
             )
-            if phase < 2:
+            if phase == 0:
                 for part in range(2):
                     started[rotation, part] = ring_start(
-                        ORDERS[rotation][1 - phase],
-                        mix_block(rotation, phase + 1),
-                        mix_land(rotation, phase + 1),
+                        ORDERS[rotation][1],
+                        mix_block(rotation, 1),
+                        mix_land(rotation, 1),
                         MIX_COLS[rotation],
                         part,
                     )
-    swapped.wait_send()
-    low, high, _ = swap_halves(attn_own)
-    out_ref[:, 0:HALF] += low
-    out_ref[:, HALF : 2 * HALF] += high
+            else:
+                started[rotation] = direct_start(
+                    ORDERS[rotation][0],
+                    mix_block(rotation, 2),
+                    mix_land(rotation, 2),
+                    whole_cols(MIX_COLS[rotation]),
+                )
+
+    def add_to_stream(cols, total):
+        stream[:, span(cols)] += total
+
+    for rotation in range(3):
+        direct_finish(
+            ORDERS[rotation][0],
+            mix_block(rotation, 2),
+            mix_land(rotation, 2),
+            whole_cols(MIX_COLS[rotation]),
+            started[rotation],
+            add_to_stream,
+        )
+    top, bottom = stream[0:4, :], stream[4:8, :]
+    swap_out[...] = jnp.where(first_core, bottom, top)
+    swapped = send(swap_out, swap_in, partner)
+    mine = jnp.where(first_core, top, bottom)
+    swapped.wait_recv()
+    theirs = swap_in[...]
+    out_ref[:, 0:HALF] = jnp.where(first_core, mine, theirs).astype(jnp.bfloat16)
+    out_ref[:, HALF : 2 * HALF] = jnp.where(first_core, theirs, mine).astype(jnp.bfloat16)
     for copy in sent:
-        if copy is not swapped:
-            copy.wait_send()
-    for token in range(4):
-        latent_copies(token).wait_send()
+        copy.wait_send()
+    latent_copies.wait_send()
 
 
 def layer(
     lengths,
     residual,
     norm_gain,
-    row_gates,
+    expert_ids,
+    gate_values,
     query_latent,
     query_rope,
     cache_latent,
@@ -670,8 +681,8 @@
     hbm = pl.BlockSpec(memory_space=pl.ANY)
     return pl.pallas_call(
         layer_kernel,
-        out_shape=jax.ShapeDtypeStruct((4, 2 * HALF), f32),
-        in_specs=[pl.BlockSpec(memory_space=pltpu.SMEM)] + [vmem] * 3 + [hbm] * 9,
+        out_shape=jax.ShapeDtypeStruct((4, 2 * HALF), bf16),
+        in_specs=[pl.BlockSpec(memory_space=pltpu.SMEM)] + [vmem] * 4 + [hbm] * 9,
         out_specs=vmem,
         scratch_shapes=[
             pltpu.VMEM(query_latent.shape, bf16),
@@ -680,43 +691,43 @@
             pltpu.VMEM(cache_rope.shape, bf16),
             pltpu.VMEM((128, 2048), f32),
             pltpu.VMEM((128, 2048), bf16),
-            pltpu.VMEM((4, 64, 2, 512), bf16),
-            pltpu.VMEM((4, 64, 2, 512), bf16),
+            pltpu.VMEM((64, 8, 512), f32),
+            pltpu.VMEM((64, 8, 512), bf16),
+            pltpu.VMEM((64, 8, 512), bf16),
             pltpu.VMEM(value_up.shape, bf16),
-            pltpu.VMEM((128, 128), f32),
-            pltpu.VMEM((128, 128), f32),
-            pltpu.VMEM((256, 128), f32),
-            pltpu.VMEM((256, 128), f32),
-            pltpu.VMEM(out_proj.shape, bf16),
+            pltpu.VMEM((512, 128), f32),
+            pltpu.VMEM((512, 128), f32),
+            pltpu.VMEM((512, HALF), bf16),
             pltpu.VMEM(w_gate.shape, bf16),
             pltpu.VMEM(w_up.shape, bf16),
-            pltpu.VMEM(w_down.shape, bf16),
-            pltpu.VMEM((4, 2, 4, 8, HALF), bf16),
-            pltpu.VMEM((4, 2, 4, 8, HALF), bf16),
+            pltpu.VMEM((512, HALF), bf16),
+            pltpu.VMEM((2, 256, 256), bf16),
             pltpu.VMEM((4, 2, 4, 8, HALF), bf16),
             pltpu.VMEM((6, 2, 4, 8, 1024), bf16),
             pltpu.VMEM((6, 4, 2, 8, 1024), bf16),
-            pltpu.VMEM((2, 6, 2, 8, 1024), bf16),
+            pltpu.VMEM((2, 3, 2, 8, 1792), bf16),
             pltpu.VMEM((8, HALF), bf16),
+            pltpu.VMEM((4, HALF), bf16),
+            pltpu.VMEM((4, HALF), bf16),
+            pltpu.VMEM((4, 128), f32),
+            pltpu.VMEM((4, 128), f32),
+            pltpu.VMEM((8, 128), f32),
+            pltpu.VMEM((8, 128), f32),
             pltpu.VMEM((8, HALF), f32),
             pltpu.VMEM((4, HALF), f32),
-            pltpu.VMEM((2, 4, HALF), f32),
-            pltpu.VMEM((2, 4, HALF + 128), bf16),
-            pltpu.VMEM((4, HALF + 128), bf16),
+            pltpu.VMEM((4, HALF), f32),
             pltpu.VMEM((2, 4, 4, 4, 8, HALF + 128), bf16),
             pltpu.VMEM((512, 256), f32),
             pltpu.VMEM((512, 256), f32),
-            pltpu.VMEM((512, 256), bf16),
-            pltpu.VMEM((4, 4, 4, 8, HALF), bf16),
-            pltpu.VMEM((4, 4, 4, 8, HALF), bf16),
+            pltpu.VMEM((2, 512, 256), bf16),
             pltpu.VMEM((4, 4, 4, 8, HALF), bf16),
             pltpu.VMEM((3, 6, 4, 4, 8, 768), bf16),
             pltpu.VMEM((3, 6, 4, 8, 768), bf16),
-            pltpu.VMEM((3, 6, 8, 768), bf16),
+            pltpu.VMEM((3, 3, 8, 1280), bf16),
             pltpu.SemaphoreType.DMA((2,)),
             pltpu.SemaphoreType.DMA((8,)),
-            pltpu.SemaphoreType.DMA((4,)),
-            pltpu.SemaphoreType.DMA((4,)),
+            pltpu.SemaphoreType.DMA((1,)),
+            pltpu.SemaphoreType.DMA((1,)),
             pltpu.SemaphoreType.DMA((170,)),
             pltpu.SemaphoreType.DMA((170,)),
         ],
@@ -727,7 +738,8 @@
         lengths,
         residual,
         norm_gain,
-        row_gates,
+        expert_ids,
+        gate_values,
         query_latent,
         query_rope,
         cache_latent,
@@ -737,7 +749,7 @@
         w_gate,
         w_up,
         w_down,
-    ).astype(bf16)
+    )
 
 
 def local(
@@ -756,15 +768,12 @@
     w_up,
     w_down,
 ):
-    experts = lax.axis_size(DEV) // 2
-    expert_range = jnp.arange(128, dtype=jnp.int32) % experts
-    chosen = expert_ids[:, :, None] == expert_range[None, None, :]
-    row_gates = jnp.sum(jnp.where(chosen, gate_values[:, :, None], 0.0), axis=1)
     return layer(
         lengths,
         residual,
         norm_gain[None, :],
-        row_gates,
+        expert_ids,
+        gate_values,
         query_latent,
         jnp.swapaxes(query_rope, 1, 2),
         cache_latent,

time: 129 us -> 115 us (0.89)
  Pallas kernels: 126 us -> 114 us
  other arithmetic: 2.91 us -> 0 us
  local copies, waits for them, and re-layouts: 0 us -> 1.46 us
    pallas_call x1, Pallas kernels: 126 us -> 114 us  [layer(): pl.pallas_call(layer_kernel, out_shape=jax.ShapeDtypeStruct((4, 2 * HALF)...]
    convert_element_type x1 -> x0, other arithmetic: 1.54 us -> none  [layer(): return pl.pallas_call(layer_kernel, out_shape=jax.ShapeDtypeStruct((4, 2...]
    unnamed x0 -> x1, local copies, waits for them, and re-layouts: none -> 1.46 us
    reduce_sum x1 -> x0, other arithmetic: 1.36 us -> none  [local(): row_gates = jnp.sum(jnp.where(chosen, gate_values[:, :, None], 0.0), axis=1)]
where the time goes in v4:
time: 115 us
  Pallas kernels  114 us (99%)
  local copies, waits for them, and re-layouts  1.46 us (1%)
    pallas_call x1, Pallas kernels, layer(): pl.pallas_call(layer_kernel, out_shape=jax.ShapeDtypeStruct((4, 2 * HALF)...  114 us

profile of v4, /device:TPU:1, one launch (start us, length us, event | category | flops | bytes accessed | tf_op | source)
XLA Modules:
  0.0 115.1 jit_solution(18156222102440935079)
XLA Ops:
  0.0 113.6 %shard_map.136 = bf16[4,7168]{1,0:T(4,128)(2,1)} custom-call(s32[4]{0:T(128)} %lengths_ref.1, bf16[4,7168]{1,0:T(4,128)(2,1)} %residual_ref.1, f32[1,7168]{1,0:T(1,128)} %bitcast.9, s32[4,8]{1,0:T(4,128)} %ids_ref.1, f32[4,8]{1,0:T(4,128)} %gate_values_ref.1, bf16[4,128,512]{2,1,0:T(8,128)(2,1)} %query_hbm.1, bf16[4,64,128]{2,1,0:T(8,128)(2,1)} %bitcast.8, ...), custom_call_target="tpu_custom_call" | custom-call | tf_op jit(solution)/shard_map/pallas_call | solution.py:682
  113.6 1.5 %copy.16 = bf16[4,7168]{1,0:T(4,128)(2,1)} copy(bf16[4,7168]{1,0:T(4,128)(2,1)} %shard_map.136) | data formatting | bytes 114688

commit v5 on v4

--- a/solution.py
+++ b/solution.py
@@ -53,6 +53,8 @@
     value_up,
     even_part,
     odd_part,
+    even_values,
+    odd_values,
     proj,
     w_gate,
     w_up,
@@ -182,6 +184,34 @@
             [jnp.where(first_core, mine, theirs), jnp.where(first_core, theirs, mine)], axis=0
         )
 
+    def scatter_pair(pair):
+        latent_out[pair] = latent_all[...].astype(jnp.bfloat16)
+
+        def scatter(step, carry):
+            number, to = peer(lax.rem(step * 19, 64))
+            pltpu.make_async_remote_copy(
+                src_ref=latent_out.at[pair, number],
+                dst_ref=latent_in.at[pair, place],
+                send_sem=latent_send.at[pair],
+                recv_sem=latent_recv.at[pair],
+                device_id=to,
+                device_id_type=MESH,
+            ).start()
+            return carry
+
+        lax.fori_loop(1, 64, scatter, 0)
+        latent_in[pair, place] = latent_out[pair, place]
+
+    def latent_copies(pair):
+        return pltpu.make_async_remote_copy(
+            src_ref=latent_out.at[pair, pl.ds(0, 63)],
+            dst_ref=latent_in.at[pair, pl.ds(0, 63)],
+            send_sem=latent_send.at[pair],
+            recv_sem=latent_recv.at[pair],
+            device_id=partner,
+            device_id_type=MESH,
+        )
+
     query_load.wait()
     query_rope_load.wait()
     loads = {}
@@ -218,7 +248,7 @@
             total = total + jnp.sum(weights, axis=1, keepdims=True)
             probs[:, cols] = weights.astype(jnp.bfloat16)
         mixed = jnp.dot(probs[...], cache[slot], preferred_element_type=jnp.float32) / total
-        latent_all[:, 2 * token : 2 * token + 2, :] = mixed.reshape(64, 2, 512)
+        latent_all[:, 2 * slot : 2 * slot + 2, :] = mixed.reshape(64, 2, 512)
         if token + 2 < 4:
             cache_loads.append(load_cache(token + 2))
         if token == 0:
@@ -234,39 +264,23 @@
             loads["up"] = load(2, up_hbm, w_up)
             loads["down"] = load(3, down_hbm.at[:, own_half], w_down.at[own_rows])
             handed["down"] = send(down_hbm.at[:, other_half], w_down.at[own_rows], partner)
-
-    latent_out[...] = latent_all[...].astype(jnp.bfloat16)
-
-    def scatter(step, carry):
-        number, to = peer(lax.rem(step * 19, 64))
-        pltpu.make_async_remote_copy(
-            src_ref=latent_out.at[number],
-            dst_ref=latent_in.at[place],
-            send_sem=latent_send.at[0],
-            recv_sem=latent_recv.at[0],
-            device_id=to,
-            device_id_type=MESH,
-        ).start()
-        return carry
-
-    lax.fori_loop(1, 64, scatter, 0)
-    latent_in[place] = latent_out[place]
-    latent_copies = pltpu.make_async_remote_copy(
-        src_ref=latent_out.at[pl.ds(0, 63)],
-        dst_ref=latent_in.at[pl.ds(0, 63)],
-        send_sem=latent_send.at[0],
-        recv_sem=latent_recv.at[0],
-        device_id=partner,
-        device_id_type=MESH,
-    )
+        if token % 2 == 1:
+            scatter_pair(token // 2)
 
     loads["value"].wait()
-    latent_copies.wait_recv()
-    latents = latent_in[...].reshape(512, 512)
-    even_part[...] = jnp.dot(latents, value_up[0], preferred_element_type=jnp.float32)
-    odd_part[...] = jnp.dot(latents, value_up[1], preferred_element_type=jnp.float32)
+    for pair in range(2):
+        latent_copies(pair).wait_recv()
+        latents = latent_in[pair].reshape(256, 512)
+        even_part[...] = jnp.dot(latents, value_up[0], preferred_element_type=jnp.float32)
+        odd_part[...] = jnp.dot(latents, value_up[1], preferred_element_type=jnp.float32)
+        for part, kept in ((even_part, even_values), (odd_part, odd_values)):
+            first = 0 if part is even_part else 1
+            heads = part[pl.ds(first, 128, stride=2), :].reshape(32, 2, 2, 128)
+            for owner in range(2):
+                at = 4 * owner + 2 * pair
+                kept[:, at : at + 2, :] = heads[:, owner]
     values[core] = jnp.concatenate(
-        [even_part[pl.ds(0, 256, stride=2), :], odd_part[pl.ds(1, 256, stride=2), :]], axis=1
+        [even_values[...].reshape(256, 128), odd_values[...].reshape(256, 128)], axis=1
     ).astype(jnp.bfloat16)
 
     def ring_start(dim, block, land, cols, part):
@@ -466,87 +480,130 @@
     for rotation in range(3):
         for copy in opened[rotation]:
             copy.wait_recv()
-    for phase in range(1, 3):
-        opened = {}
-        for rotation in range(3):
-            dims = ORDERS[rotation]
-            dim = dims[phase]
-            first, second = GATHER_COLS[rotation]
-            fixed = {later: pos[later] for later in dims[phase:]}
-            up, down = device(dim, above(dim)), device(dim, below(dim))
-            one, two = row_block(fixed, first), row_block(fixed, second)
-            opened[rotation] = (
-                send(one, one, up),
-                send(two, two, down),
-                send(two, two, up),
-                send(one, one, down),
-            )
-            if phase == 2:
-                whole = row_block(fixed, (first[0], first[1] + second[1]))
-                shared.append(send(whole, whole, partner))
-        forwarded = {}
-        for rotation in range(3):
-            dims = ORDERS[rotation]
-            dim = dims[phase]
-            first, second = GATHER_COLS[rotation]
-            fixed = {later: pos[later] for later in dims[phase:]}
-            up, down = device(dim, above(dim)), device(dim, below(dim))
-            opened[rotation][0].wait_recv()
-            one = row_block({**fixed, dim: below(dim)}, first)
-            opened[rotation][1].wait_recv()
-            two = row_block({**fixed, dim: above(dim)}, second)
-            forwarded[rotation] = (send(one, one, up), send(two, two, down))
-        for rotation in range(3):
-            dims = ORDERS[rotation]
-            dim = dims[phase]
-            first, second = GATHER_COLS[rotation]
-            fixed = {later: pos[later] for later in dims[phase:]}
-            opened[rotation][2].wait_recv()
-            opened[rotation][3].wait_recv()
-            if phase == 2:
-                for place in (below(dim), above(dim)):
-                    whole = row_block({**fixed, dim: place}, (first[0], first[1] + second[1]))
-                    shared.append(send(whole, whole, partner))
-        for rotation in range(3):
-            dims = ORDERS[rotation]
-            dim = dims[phase]
-            first, second = GATHER_COLS[rotation]
-            fixed = {later: pos[later] for later in dims[phase:]}
-            forwarded[rotation][0].wait_recv()
-            forwarded[rotation][1].wait_recv()
-            if phase == 2:
-                whole = row_block({**fixed, dim: across(dim)}, (first[0], first[1] + second[1]))
-                shared.append(send(whole, whole, partner))
-    for copy in shared:
-        copy.wait_recv()
-
+    def gather_dims(rotation):
+        first, second = GATHER_COLS[rotation]
+        return ORDERS[rotation], first, second
+
+    def open_ring(dim, at, first, second):
+        up, down = device(dim, above(dim)), device(dim, below(dim))
+        one, two = row_block(at, first), row_block(at, second)
+        return (
+            send(one, one, up),
+            send(two, two, down),
+            send(two, two, up),
+            send(one, one, down),
+        )
+
+    def forward(dim, at, first, second, begun):
+        begun[0].wait_recv()
+        one = row_block({**at, dim: below(dim)}, first)
+        upward = send(one, one, device(dim, above(dim)))
+        begun[1].wait_recv()
+        two = row_block({**at, dim: above(dim)}, second)
+        return upward, send(two, two, device(dim, below(dim)))
+
+    def hand_over(rotation, at):
+        piece = row_block(at, whole_cols(GATHER_COLS[rotation]))
+        return send(piece, piece, partner)
+
+    middle, outer, passed, shared = {}, {}, {}, {}
+    for rotation in range(3):
+        (a, b, c), first, second = gather_dims(rotation)
+        middle[rotation] = open_ring(b, {b: pos[b], c: pos[c]}, first, second)
+    for rotation in range(3):
+        (a, b, c), first, second = gather_dims(rotation)
+        at = {b: pos[b], c: pos[c]}
+        outer[rotation, "own"] = open_ring(c, at, first, second)
+    for rotation in range(3):
+        (a, b, c), first, second = gather_dims(rotation)
+        passed[rotation] = forward(b, {c: pos[c]}, first, second, middle[rotation])
+    for rotation in range(3):
+        (a, b, c), first, second = gather_dims(rotation)
+        middle[rotation][2].wait_recv()
+        middle[rotation][3].wait_recv()
+        for where in (below, above):
+            outer[rotation, where] = open_ring(c, {b: where(b), c: pos[c]}, first, second)
+    onward = {}
+    for rotation in range(3):
+        (a, b, c), first, second = gather_dims(rotation)
+        onward[rotation, "own"] = forward(c, {b: pos[b]}, first, second, outer[rotation, "own"])
+    for rotation in range(3):
+        (a, b, c), first, second = gather_dims(rotation)
+        passed[rotation][0].wait_recv()
+        passed[rotation][1].wait_recv()
+        outer[rotation, across] = open_ring(c, {b: across(b), c: pos[c]}, first, second)
+        shared[rotation, "own"] = [hand_over(rotation, {c: pos[c]})]
     loads["gate"].wait()
     loads["up"].wait()
+
+    def acc_rows(acc, at):
+        return acc.at[at.get("x", slice(None)), at.get("y", slice(None)), at.get("z", slice(None))]
+
+    def multiply(half, rotation, at):
+        start = GATHER_COLS[rotation][0][0]
+        depth = min(whole_cols(GATHER_COLS[rotation])[1], HALF - start)
+        index = (at.get("x", slice(None)), at.get("y", slice(None)), at.get("z", slice(None)))
+        lhs = rows[(half,) + index + (slice(None), pl.ds(start, depth))].reshape(128, depth)
+        weight_rows = pl.ds(pl.multiple_of(half * HALF + start, 128), depth)
+        for acc, weight in ((gate_acc, w_gate), (up_acc, w_up)):
+            part = jnp.dot(
+                lhs, weight[weight_rows, :], preferred_element_type=jnp.float32
+            ).reshape(4, 4, 8, 256)
+            acc_rows(acc, at)[...] += part
+
     gate_acc[...] = jnp.zeros_like(gate_acc)
     up_acc[...] = jnp.zeros_like(up_acc)
-    depth = 512
-    for half in range(2):
-
-        def product(step, carry):
-            at = pl.multiple_of(step * depth, depth)
-            row = pl.multiple_of(half * HALF + step * depth, depth)
-            lhs = rows[half, :, :, :, :, pl.ds(at, depth)].reshape(512, depth)
-            gate_acc[...] += jnp.dot(
-                lhs, w_gate[pl.ds(row, depth), :], preferred_element_type=jnp.float32
-            )
-            up_acc[...] += jnp.dot(
-                lhs, w_up[pl.ds(row, depth), :], preferred_element_type=jnp.float32
-            )
-            return carry
-
-        lax.fori_loop(0, HALF // depth, product, 0)
+    for rotation in range(3):
+        c = ORDERS[rotation][2]
+        multiply(core, rotation, {c: pos[c]})
+    for name, where in (("below", below), ("above", above), ("across", across)):
+        for rotation in range(3):
+            (a, b, c), first, second = gather_dims(rotation)
+            onward[rotation, name] = forward(c, {b: where(b)}, first, second, outer[rotation, where])
+    for rotation in range(3):
+        c = ORDERS[rotation][2]
+        shared[rotation, "own"][0].wait_recv()
+        multiply(other, rotation, {c: pos[c]})
+    for rotation in range(3):
+        c = ORDERS[rotation][2]
+        for key in ("own", below, above, across):
+            outer[rotation, key][2].wait_recv()
+            outer[rotation, key][3].wait_recv()
+        for where in (below, above):
+            shared[rotation, where] = [hand_over(rotation, {c: where(c)})]
+    for where in (below, above):
+        for rotation in range(3):
+            c = ORDERS[rotation][2]
+            multiply(core, rotation, {c: where(c)})
+    for rotation in range(3):
+        b, c = ORDERS[rotation][1:]
+        shared[rotation, across] = []
+        for name, there in (("own", None), ("below", below), ("above", above), ("across", across)):
+            for copy in onward[rotation, name]:
+                copy.wait_recv()
+            at = {c: across(c), b: pos[b] if there is None else there(b)}
+            shared[rotation, across].append(hand_over(rotation, at))
+    for where in (below, above):
+        for rotation in range(3):
+            c = ORDERS[rotation][2]
+            shared[rotation, where][0].wait_recv()
+            multiply(other, rotation, {c: where(c)})
+    for rotation in range(3):
+        c = ORDERS[rotation][2]
+        multiply(core, rotation, {c: across(c)})
+    for rotation in range(3):
+        c = ORDERS[rotation][2]
+        for copy in shared[rotation, across]:
+            copy.wait_recv()
+        multiply(other, rotation, {c: across(c)})
+
     expert = (pos["z"] * 2 + x_lo) * 4 + pos["y"]
     parts = rows[0, :, :, :, :, HALF : HALF + 128].astype(jnp.float32).reshape(512, 128)
     lane = lax.broadcasted_iota(jnp.int32, parts.shape, 1)
     picked = jnp.where((lane == expert) | (lane == expert + 32), parts, 0.0)
     row_gate = jnp.sum(picked, axis=1, keepdims=True)
-    gate_part = gate_acc[...]
-    active[core] = (gate_part * jax.nn.sigmoid(gate_part) * up_acc[...] * row_gate).astype(
+    gate_part = gate_acc[...].reshape(512, 256)
+    active[core] = (gate_part * jax.nn.sigmoid(gate_part) * up_acc[...].reshape(512, 256) * row_gate).astype(
         jnp.bfloat16
     )
 
@@ -583,7 +640,17 @@
 
         return place
 
-    started = {}
+    started, relayed = {}, {}
+
+    def mix_relay(rotation, phase):
+        relayed[rotation] = ring_relay(
+            ORDERS[rotation][2 - phase],
+            mix_block(rotation, phase),
+            mix_land(rotation, phase),
+            MIX_COLS[rotation],
+            (started[rotation, 0], started[rotation, 1]),
+        )
+
     for rotation in range(3):
         for part in range(2):
             cols = MIX_COLS[rotation][part]
@@ -596,16 +663,13 @@
             started[rotation, part] = ring_start(
                 ORDERS[rotation][2], mix_block(rotation, 0), mix_land(rotation, 0), MIX_COLS[rotation], part
             )
+        if rotation >= 1:
+            mix_relay(rotation - 1, 0)
+    mix_relay(2, 0)
     for phase in range(2):
-        relayed = {}
-        for rotation in range(3):
-            relayed[rotation] = ring_relay(
-                ORDERS[rotation][2 - phase],
-                mix_block(rotation, phase),
-                mix_land(rotation, phase),
-                MIX_COLS[rotation],
-                (started[rotation, 0], started[rotation, 1]),
-            )
+        if phase == 1:
+            for rotation in range(3):
+                mix_relay(rotation, 1)
         for rotation in range(3):
             dim = ORDERS[rotation][2 - phase]
             block = mix_block(rotation, phase)
@@ -657,7 +721,8 @@
     out_ref[:, HALF : 2 * HALF] = jnp.where(first_core, theirs, mine).astype(jnp.bfloat16)
     for copy in sent:
         copy.wait_send()
-    latent_copies.wait_send()
+    for pair in range(2):
+        latent_copies(pair).wait_send()
 
 
 def layer(
@@ -691,12 +756,14 @@
             pltpu.VMEM(cache_rope.shape, bf16),
             pltpu.VMEM((128, 2048), f32),
             pltpu.VMEM((128, 2048), bf16),
-            pltpu.VMEM((64, 8, 512), f32),
-            pltpu.VMEM((64, 8, 512), bf16),
-            pltpu.VMEM((64, 8, 512), bf16),
+            pltpu.VMEM((64, 4, 512), f32),
+            pltpu.VMEM((2, 64, 4, 512), bf16),
+            pltpu.VMEM((2, 64, 4, 512), bf16),
             pltpu.VMEM(value_up.shape, bf16),
-            pltpu.VMEM((512, 128), f32),
-            pltpu.VMEM((512, 128), f32),
+            pltpu.VMEM((256, 128), f32),
+            pltpu.VMEM((256, 128), f32),
+            pltpu.VMEM((32, 8, 128), f32),
+            pltpu.VMEM((32, 8, 128), f32),
             pltpu.VMEM((512, HALF), bf16),
             pltpu.VMEM(w_gate.shape, bf16),
             pltpu.VMEM(w_up.shape, bf16),
@@ -717,8 +784,8 @@
             pltpu.VMEM((4, HALF), f32),
             pltpu.VMEM((4, HALF), f32),
             pltpu.VMEM((2, 4, 4, 4, 8, HALF + 128), bf16),
-            pltpu.VMEM((512, 256), f32),
-            pltpu.VMEM((512, 256), f32),
+            pltpu.VMEM((4, 4, 4, 8, 256), f32),
+            pltpu.VMEM((4, 4, 4, 8, 256), f32),
             pltpu.VMEM((2, 512, 256), bf16),
             pltpu.VMEM((4, 4, 4, 8, HALF), bf16),
             pltpu.VMEM((3, 6, 4, 4, 8, 768), bf16),
@@ -726,10 +793,10 @@
             pltpu.VMEM((3, 3, 8, 1280), bf16),
             pltpu.SemaphoreType.DMA((2,)),
             pltpu.SemaphoreType.DMA((8,)),
-            pltpu.SemaphoreType.DMA((1,)),
-            pltpu.SemaphoreType.DMA((1,)),
-            pltpu.SemaphoreType.DMA((170,)),
-            pltpu.SemaphoreType.DMA((170,)),
+            pltpu.SemaphoreType.DMA((2,)),
+            pltpu.SemaphoreType.DMA((2,)),
+            pltpu.SemaphoreType.DMA((240,)),
+            pltpu.SemaphoreType.DMA((240,)),
         ],
         compiler_params=pltpu.CompilerParams(
             collective_id=0, has_side_effects=True, vmem_limit_bytes=63 * 1024 * 1024

time: 115 us -> 115 us (level)
  no operation moved by 1% of the time
where the time goes in v5:
time: 115 us
  Pallas kernels  113 us (98%)
  local copies, waits for them, and re-layouts  1.46 us (1%)
    pallas_call x1, Pallas kernels, layer(): pl.pallas_call(layer_kernel, out_shape=jax.ShapeDtypeStruct((4, 2 * HALF)...  113 us

profile of v5, /device:TPU:1, one launch (start us, length us, event | category | flops | bytes accessed | tf_op | source)
XLA Modules:
  0.0 114.6 jit_solution(249519734645303905)
XLA Ops:
  0.0 113.2 %shard_map.136 = bf16[4,7168]{1,0:T(4,128)(2,1)} custom-call(s32[4]{0:T(128)} %lengths_ref.1, bf16[4,7168]{1,0:T(4,128)(2,1)} %residual_ref.1, f32[1,7168]{1,0:T(1,128)} %bitcast.9, s32[4,8]{1,0:T(4,128)} %ids_ref.1, f32[4,8]{1,0:T(4,128)} %gate_values_ref.1, bf16[4,128,512]{2,1,0:T(8,128)(2,1)} %query_hbm.1, bf16[4,64,128]{2,1,0:T(8,128)(2,1)} %bitcast.8, ...), custom_call_target="tpu_custom_call" | custom-call | tf_op jit(solution)/shard_map/pallas_call | solution.py:747
  113.2 1.5 %copy.16 = bf16[4,7168]{1,0:T(4,128)(2,1)} copy(bf16[4,7168]{1,0:T(4,128)(2,1)} %shard_map.136) | data formatting | bytes 114688

commit v6 on v5

--- a/solution.py
+++ b/solution.py
@@ -18,10 +18,10 @@
 
 HALF = 3584
 UNIT = 256
-ATTN_COLS = (((0, 1024), (1024, 768)), ((1792, 1024), (2816, 768)))
+ATTN_COLS = (((0, 896), (896, 896)), ((1792, 896), (2688, 896)))
 ATTN_ORDERS = (("z", "y"), ("y", "z"))
 GATHER_COLS = (((0, 640), (640, 640)), ((1280, 640), (1920, 640)), ((2560, 640), (3200, 512)))
-MIX_COLS = (((0, 768), (768, 512)), ((1280, 768), (2048, 512)), ((2560, 512), (3072, 512)))
+MIX_COLS = (((0, 640), (640, 512)), ((1152, 640), (1792, 640)), ((2432, 640), (3072, 512)))
 ORDERS = (("z", "y", "x"), ("y", "x", "z"), ("x", "z", "y"))
 
 
@@ -251,14 +251,13 @@
         latent_all[:, 2 * slot : 2 * slot + 2, :] = mixed.reshape(64, 2, 512)
         if token + 2 < 4:
             cache_loads.append(load_cache(token + 2))
-        if token == 0:
+        if token == 1:
             pl.semaphore_wait(barrier, 65)
             handed = {
                 "residual": send(residual_out, residual_in, partner),
                 "gates": send(gates_out, gates_in, partner),
                 "proj": send(proj_hbm.at[:, other_half], proj.at[own_rows], partner),
             }
-        elif token == 1:
             loads["gate"] = load(1, gate_hbm, w_gate)
         elif token == 2:
             loads["up"] = load(2, up_hbm, w_up)
@@ -375,11 +374,12 @@
         for part in range(2):
             cols = ATTN_COLS[rotation][part]
             for start in range(cols[0], cols[0] + cols[1], UNIT):
-                piece = pl.ds(start, UNIT)
+                width = min(UNIT, cols[0] + cols[1] - start)
+                piece = pl.ds(start, width)
                 share = jnp.dot(
                     values[0], proj[0:256, piece], preferred_element_type=jnp.float32
                 ) + jnp.dot(values[1], proj[256:512, piece], preferred_element_type=jnp.float32)
-                attn_sum[:, :, :, :, piece] = share.reshape(4, 2, 4, 8, UNIT).astype(jnp.bfloat16)
+                attn_sum[:, :, :, :, piece] = share.reshape(4, 2, 4, 8, width).astype(jnp.bfloat16)
             started[rotation, part] = ring_start(
                 ATTN_ORDERS[rotation][0],
                 attn_block(rotation, 0),
@@ -655,17 +655,17 @@
         for part in range(2):
             cols = MIX_COLS[rotation][part]
             for start in range(cols[0], cols[0] + cols[1], UNIT):
-                piece = pl.ds(start, UNIT)
+                width = min(UNIT, cols[0] + cols[1] - start)
+                piece = pl.ds(start, width)
                 share = jnp.dot(
                     active[0], w_down[0:256, piece], preferred_element_type=jnp.float32
                 ) + jnp.dot(active[1], w_down[256:512, piece], preferred_element_type=jnp.float32)
-                mix_sum[:, :, :, :, piece] = share.reshape(4, 4, 4, 8, UNIT).astype(jnp.bfloat16)
+                mix_sum[:, :, :, :, piece] = share.reshape(4, 4, 4, 8, width).astype(jnp.bfloat16)
             started[rotation, part] = ring_start(
                 ORDERS[rotation][2], mix_block(rotation, 0), mix_land(rotation, 0), MIX_COLS[rotation], part
             )
-        if rotation >= 1:
-            mix_relay(rotation - 1, 0)
-    mix_relay(2, 0)
+    for rotation in range(3):
+        mix_relay(rotation, 0)
     for phase in range(2):
         if phase == 1:
             for rotation in range(3):

time: 115 us -> 109 us (0.948)
  Pallas kernels: 113 us -> 107 us
    pallas_call x1, Pallas kernels: 113 us -> 107 us  [layer(): pl.pallas_call(layer_kernel, out_shape=jax.ShapeDtypeStruct((4, 2 * HALF)...]
where the time goes in v6:
time: 109 us
  Pallas kernels  107 us (98%)
  local copies, waits for them, and re-layouts  1.46 us (1%)
    pallas_call x1, Pallas kernels, layer(): pl.pallas_call(layer_kernel, out_shape=jax.ShapeDtypeStruct((4, 2 * HALF)...  107 us

profile of v6, /device:TPU:1, one launch (start us, length us, event | category | flops | bytes accessed | tf_op | source)
XLA Modules:
  0.0 108.9 jit_solution(13461969585779194768)
XLA Ops:
  0.0 107.5 %shard_map.136 = bf16[4,7168]{1,0:T(4,128)(2,1)} custom-call(s32[4]{0:T(128)} %lengths_ref.1, bf16[4,7168]{1,0:T(4,128)(2,1)} %residual_ref.1, f32[1,7168]{1,0:T(1,128)} %bitcast.9, s32[4,8]{1,0:T(4,128)} %ids_ref.1, f32[4,8]{1,0:T(4,128)} %gate_values_ref.1, bf16[4,128,512]{2,1,0:T(8,128)(2,1)} %query_hbm.1, bf16[4,64,128]{2,1,0:T(8,128)(2,1)} %bitcast.8, ...), custom_call_target="tpu_custom_call" | custom-call | tf_op jit(solution)/shard_map/pallas_call | solution.py:747
  107.5 1.5 %copy.16 = bf16[4,7168]{1,0:T(4,128)(2,1)} copy(bf16[4,7168]{1,0:T(4,128)(2,1)} %shard_map.136) | data formatting | bytes 114688

commit v7 on v6

--- a/solution.py
+++ b/solution.py
@@ -640,16 +640,41 @@
 
         return place
 
+    subs = {"across": across, "below": below, "above": above, "own": lambda dim: pos[dim]}
+    order = tuple(subs)
     started, relayed = {}, {}
 
-    def mix_relay(rotation, phase):
-        relayed[rotation] = ring_relay(
-            ORDERS[rotation][2 - phase],
-            mix_block(rotation, phase),
-            mix_land(rotation, phase),
-            MIX_COLS[rotation],
-            (started[rotation, 0], started[rotation, 1]),
-        )
+    def sub_block(rotation, name):
+        b, c = ORDERS[rotation][1:]
+
+        def block(where, cols):
+            at = {c: where, b: subs[name](b)}
+            index = tuple(at.get(dim, slice(None)) for dim in ("x", "y", "z"))
+            return mix_sum.at[index + (slice(None), span(cols))]
+
+        def land(slot, cols):
+            at = {b: subs[name](b)}
+            index = tuple(at.get(dim, slice(None)) for dim in ("x", "y", "z") if dim != c)
+            return mix_land0.at[(rotation, slot) + index + (slice(None), pl.ds(0, cols[1]))]
+
+        return c, block, land, MIX_COLS[rotation]
+
+    def sub_relayed_part(rotation, name, part):
+        dim, block, land, cols = sub_block(rotation, name)
+        way = above(dim) if part == 0 else below(dim)
+        piece = block(across(dim), cols[part])
+        return send(piece, land(2 * part, cols[part]), device(dim, way))
+
+    def sub_direct_part(rotation, name, part):
+        dim, block, land, cols = sub_block(rotation, name)
+        way = below(dim) if part == 0 else above(dim)
+        piece = block(way, cols[part])
+        return send(piece, land(2 * part + 1, cols[part]), device(dim, way))
+
+    def sub_finish(rotation, name):
+        dim, block, land, cols = sub_block(rotation, name)
+        begun = tuple(started[rotation, name, part] for part in range(2))
+        ring_finish(dim, block, land, cols, begun, relayed[rotation, name], keep_in(block, dim))
 
     for rotation in range(3):
         for part in range(2):
@@ -661,43 +686,67 @@
                     active[0], w_down[0:256, piece], preferred_element_type=jnp.float32
                 ) + jnp.dot(active[1], w_down[256:512, piece], preferred_element_type=jnp.float32)
                 mix_sum[:, :, :, :, piece] = share.reshape(4, 4, 4, 8, width).astype(jnp.bfloat16)
-            started[rotation, part] = ring_start(
-                ORDERS[rotation][2], mix_block(rotation, 0), mix_land(rotation, 0), MIX_COLS[rotation], part
-            )
-    for rotation in range(3):
-        mix_relay(rotation, 0)
-    for phase in range(2):
-        if phase == 1:
-            for rotation in range(3):
-                mix_relay(rotation, 1)
+            for name in order:
+                started[rotation, name, part] = [sub_relayed_part(rotation, name, part)]
+            started[rotation, "across", part].append(sub_direct_part(rotation, "across", part))
+
+    middle = {}
+    for number, name in enumerate(order):
         for rotation in range(3):
-            dim = ORDERS[rotation][2 - phase]
-            block = mix_block(rotation, phase)
-            ring_finish(
-                dim,
-                block,
-                mix_land(rotation, phase),
-                MIX_COLS[rotation],
-                (started[rotation, 0], started[rotation, 1]),
-                relayed[rotation],
-                keep_in(block, dim),
-            )
-            if phase == 0:
+            dim, block, land, cols = sub_block(rotation, name)
+            begun = tuple(started[rotation, name, part] for part in range(2))
+            relayed[rotation, name] = ring_relay(dim, block, land, cols, begun)
+            if number < 3:
                 for part in range(2):
-                    started[rotation, part] = ring_start(
-                        ORDERS[rotation][1],
-                        mix_block(rotation, 1),
-                        mix_land(rotation, 1),
-                        MIX_COLS[rotation],
-                        part,
+                    started[rotation, order[number + 1], part].append(
+                        sub_direct_part(rotation, order[number + 1], part)
                     )
+        if number == 0:
+            continue
+        ready = order[number - 1]
+        for rotation in range(3):
+            sub_finish(rotation, ready)
+            b = ORDERS[rotation][1]
+            block, land = mix_block(rotation, 1), mix_land(rotation, 1)
+            first, second = MIX_COLS[rotation]
+            up, down = device(b, above(b)), device(b, below(b))
+            if ready == "across":
+                middle[rotation] = (
+                    [send(block(across(b), first), land(0, first), up)],
+                    [send(block(across(b), second), land(2, second), down)],
+                )
+            elif ready == "below":
+                middle[rotation][0].append(send(block(below(b), first), land(1, first), down))
             else:
-                started[rotation] = direct_start(
-                    ORDERS[rotation][0],
-                    mix_block(rotation, 2),
-                    mix_land(rotation, 2),
-                    whole_cols(MIX_COLS[rotation]),
-                )
+                middle[rotation][1].append(send(block(above(b), second), land(3, second), up))
+    for rotation in range(3):
+        relayed[rotation] = ring_relay(
+            ORDERS[rotation][1],
+            mix_block(rotation, 1),
+            mix_land(rotation, 1),
+            MIX_COLS[rotation],
+            middle[rotation],
+        )
+    for rotation in range(3):
+        sub_finish(rotation, "own")
+    for rotation in range(3):
+        dim = ORDERS[rotation][1]
+        block = mix_block(rotation, 1)
+        ring_finish(
+            dim,
+            block,
+            mix_land(rotation, 1),
+            MIX_COLS[rotation],
+            middle[rotation],
+            relayed[rotation],
+            keep_in(block, dim),
+        )
+        started[rotation] = direct_start(
+            ORDERS[rotation][0],
+            mix_block(rotation, 2),
+            mix_land(rotation, 2),
+            whole_cols(MIX_COLS[rotation]),
+        )
 
     def add_to_stream(cols, total):
         stream[:, span(cols)] += total
@@ -795,8 +844,8 @@
             pltpu.SemaphoreType.DMA((8,)),
             pltpu.SemaphoreType.DMA((2,)),
             pltpu.SemaphoreType.DMA((2,)),
-            pltpu.SemaphoreType.DMA((240,)),
-            pltpu.SemaphoreType.DMA((240,)),
+            pltpu.SemaphoreType.DMA((260,)),
+            pltpu.SemaphoreType.DMA((260,)),
         ],
         compiler_params=pltpu.CompilerParams(
             collective_id=0, has_side_effects=True, vmem_limit_bytes=63 * 1024 * 1024

time: 109 us -> 105 us (0.963)
  Pallas kernels: 107 us -> 103 us
    pallas_call x1, Pallas kernels: 107 us -> 103 us  [layer(): pl.pallas_call(layer_kernel, out_shape=jax.ShapeDtypeStruct((4, 2 * HALF)...]
where the time goes in v7:
time: 105 us
  Pallas kernels  103 us (98%)
  local copies, waits for them, and re-layouts  1.46 us (1%)
    pallas_call x1, Pallas kernels, layer(): pl.pallas_call(layer_kernel, out_shape=jax.ShapeDtypeStruct((4, 2 * HALF)...  103 us

profile of v7, /device:TPU:1, one launch (start us, length us, event | category | flops | bytes accessed | tf_op | source)
XLA Modules:
  0.0 104.7 jit_solution(7038253057256340506)
XLA Ops:
  0.0 103.3 %shard_map.136 = bf16[4,7168]{1,0:T(4,128)(2,1)} custom-call(s32[4]{0:T(128)} %lengths_ref.1, bf16[4,7168]{1,0:T(4,128)(2,1)} %residual_ref.1, f32[1,7168]{1,0:T(1,128)} %bitcast.9, s32[4,8]{1,0:T(4,128)} %ids_ref.1, f32[4,8]{1,0:T(4,128)} %gate_values_ref.1, bf16[4,128,512]{2,1,0:T(8,128)(2,1)} %query_hbm.1, bf16[4,64,128]{2,1,0:T(8,128)(2,1)} %bitcast.8, ...), custom_call_target="tpu_custom_call" | custom-call | tf_op jit(solution)/shard_map/pallas_call | solution.py:796
  103.3 1.5 %copy.16 = bf16[4,7168]{1,0:T(4,128)(2,1)} copy(bf16[4,7168]{1,0:T(4,128)(2,1)} %shard_map.136) | data formatting | bytes 114688
